TPU v7x, 128 devices: a whole 4x4x4 slice. The times are simulated.
128 devices in a mesh: dp: 4 (over y), ctx: 32 (over x, z, core).
Axes of the slice: x: 4, y: 4, z: 4, core: 2. Of those that a mesh axis runs over, the one named last changes fastest.
Arguments:
- x_in: bfloat16 [4, 4096, 4096], P('dp', 'ctx'), may hold values from -6 to 6
- b_in: bfloat16 [4, 4096, 128], P('dp', 'ctx'), may hold values from -6 to 6
- c_in: bfloat16 [4, 4096, 128], P('dp', 'ctx'), may hold values from -6 to 6
- log_decay: int32 [4, 4096, 64], P('dp', 'ctx'), may hold values from 0 to 14000, as said below
- w_out: bfloat16 [4096, 2048], P(('dp', 'ctx')), may hold values from -0.09375 to 0.09375
- cotangent: bfloat16 [4, 4096, 2048], P('dp', 'ctx'), may hold values from -6 to 6
Outputs:
- out: bfloat16 [4, 4096, 2048], P('dp', 'ctx')
- grad_x: bfloat16 [4, 4096, 4096], P('dp', 'ctx')
- grad_b: bfloat16 [4, 4096, 128], P('dp', 'ctx')
- gradient_c_input: bfloat16 [4, 4096, 128], P('dp', 'ctx')
Inputs may be any that keep to these rules, and one draw needn't show every extreme that they name: log_decay holds each head's per-token log-decay as a whole number.
All inputs are finite; a program needn't handle non-finite values.
Results may differ from a plain program's by a relative error of at most 0.01.
Values may be sent and summed in bfloat16 or wider, within the bound.
A program may use at most 320 MiB of HBM per device.

v0:
```python
import jax
import jax.numpy as jnp
from jax import lax
from jax.sharding import PartitionSpec as P

decay_unit = 5e-05


def causal_decay(local_group):
    cum = local_group.T
    rows = cum.shape[1]
    diff = (cum[:, :, None] - cum[:, None, :]).astype(jnp.float32)
    lower = lax.broadcasted_iota(jnp.int32, (rows, rows), 0) >= lax.broadcasted_iota(
        jnp.int32, (rows, rows), 1
    )
    return jnp.where(lower[None], jnp.exp(-decay_unit * diff), jnp.float32(0.0))


def forward_inside_group(x_bf, local, scores, scale, group, width):
    rows, inner = x_bf.shape
    heads = local.shape[1]
    count = heads // group
    x_groups = x_bf.reshape(rows, count, group, width).transpose(1, 0, 2, 3)
    l_groups = local.reshape(rows, count, group).transpose(1, 0, 2)

    def forward_one_group(carry, item):
        x_part, l_part = item
        mix = (scale * scores[None] * causal_decay(l_part)).astype(jnp.bfloat16)
        part = jnp.einsum("gtr,rgp->tgp", mix, x_part, preferred_element_type=jnp.float32)
        return (carry, (mix, part))

    _, (mixes, parts) = lax.scan(
        forward_one_group, jnp.zeros((), jnp.float32), (x_groups, l_groups)
    )
    return (mixes, parts.transpose(1, 0, 2, 3).reshape(rows, inner))


def backward_intra(mixes, x_bf, back_bf, local, scale, group, width):
    rows, inner = x_bf.shape
    heads = local.shape[1]
    count = heads // group
    x_groups = x_bf.reshape(rows, count, group, width).transpose(1, 0, 2, 3)
    d_groups = back_bf.reshape(rows, count, group, width).transpose(1, 0, 2, 3)
    l_groups = local.reshape(rows, count, group).transpose(1, 0, 2)

    def backward_one_group(total, item):
        mix, x_part, d_part, l_part = item
        flowed = jnp.einsum("gtr,tgp->rgp", mix, d_part, preferred_element_type=jnp.float32)
        inner_prod = jnp.einsum("tgp,rgp->gtr", d_part, x_part, preferred_element_type=jnp.float32)
        total = total + jnp.sum(scale * causal_decay(l_part) * inner_prod, axis=0)
        return (total, flowed)

    kernel, flows = lax.scan(
        backward_one_group,
        jnp.zeros((rows, rows), jnp.float32),
        (mixes, x_groups, d_groups, l_groups),
    )
    return (kernel, flows.transpose(1, 0, 2, 3).reshape(rows, inner))


def body(x_in, b_in, c_in, log_decay, w_out, cotangent):
    x_bf = x_in[0]
    b_blk = b_in[0]
    c_blk = c_in[0]
    steps = log_decay[0]
    grad_out = cotangent[0]
    rows, inner = x_bf.shape
    heads = steps.shape[1]
    width = inner // heads
    length = rows * lax.axis_size("ctx")
    scale = (b_blk.shape[1] * length) ** (-0.5)
    group = 8
    local = jnp.cumsum(steps, axis=0)
    totals = local[-1]
    fall_wide = jnp.repeat(jnp.exp(-decay_unit * local.astype(jnp.float32)), width, axis=1)
    tail_wide = jnp.repeat(
        jnp.exp(-decay_unit * (totals[None, :] - local).astype(jnp.float32)), width, axis=1
    )
    scores = jnp.dot(c_blk, b_blk.T, preferred_element_type=jnp.float32)
    mixes, y_intra = forward_inside_group(x_bf, local, scores, scale, group, width)
    shifted = (x_bf * tail_wide).astype(jnp.bfloat16)
    term = jnp.dot(b_blk.T, shifted, preferred_element_type=jnp.float32)
    mine = lax.axis_index("ctx")
    all_totals = lax.all_gather(totals[None, :], "ctx", axis=0, tiled=True)
    before_sum = jnp.cumsum(all_totals, axis=0) - all_totals
    mine_before = lax.dynamic_slice_in_dim(before_sum, mine, 1, 0)
    mine_total = lax.dynamic_slice_in_dim(all_totals, mine, 1, 0)

    def weighted_add(carry, piece, later):
        count = piece.shape[0]
        index_set = jnp.arange(count, dtype=jnp.int32)
        if later:
            span = before_sum - mine_before - mine_total
            live = index_set > mine
        else:
            span = mine_before - before_sum - all_totals
            live = index_set < mine
        span = jnp.maximum(span, 0).astype(jnp.float32)
        weight = jnp.where(live[:, None], jnp.exp(-decay_unit * span), jnp.float32(0.0))
        weight_wide = jnp.repeat(weight, width, axis=1)
        return carry + jnp.einsum("ksi,ki->si", piece, weight_wide, precision=lax.Precision.HIGHEST)

    before = weighted_add(
        jnp.zeros_like(term), lax.all_gather(term[None], "ctx", axis=0, tiled=True), False
    )
    before_bf = before.astype(jnp.bfloat16)
    mixed = (
        y_intra + scale * fall_wide * jnp.dot(c_blk, before_bf, preferred_element_type=jnp.float32)
    ).astype(jnp.bfloat16)
    whole_proj = lax.all_gather(w_out, ("dp", "ctx"), axis=0, tiled=True)
    out = jnp.dot(mixed, whole_proj, preferred_element_type=jnp.float32).astype(jnp.bfloat16)
    back_bf = lax.dot_general(
        grad_out, whole_proj, (((1,), (1,)), ((), ())), preferred_element_type=jnp.float32
    ).astype(jnp.bfloat16)
    dshift = (back_bf * fall_wide).astype(jnp.bfloat16)
    adjoint_term = jnp.dot(c_blk.T, dshift, preferred_element_type=jnp.float32)
    after = weighted_add(
        jnp.zeros_like(adjoint_term),
        lax.all_gather(adjoint_term[None].astype(jnp.bfloat16), "ctx", axis=0, tiled=True).astype(
            jnp.float32
        ),
        True,
    )
    after_bf = after.astype(jnp.bfloat16)
    kernel, dx_intra = backward_intra(mixes, x_bf, back_bf, local, scale, group, width)
    kernel_bf = kernel.astype(jnp.bfloat16)
    grad_x = (
        dx_intra + scale * tail_wide * jnp.dot(b_blk, after_bf, preferred_element_type=jnp.float32)
    ).astype(jnp.bfloat16)
    grad_b = (
        jnp.dot(kernel_bf.T, c_blk, preferred_element_type=jnp.float32)
        + scale * jnp.dot(shifted, after_bf.T, preferred_element_type=jnp.float32)
    ).astype(jnp.bfloat16)
    gradient_c_input = (
        jnp.dot(kernel_bf, b_blk, preferred_element_type=jnp.float32)
        + scale * jnp.dot(dshift, before_bf.T, preferred_element_type=jnp.float32)
    ).astype(jnp.bfloat16)
    return (out[None], grad_x[None], grad_b[None], gradient_c_input[None])


def solution(mesh):
    in_specs = (
        P("dp", "ctx", None),
        P("dp", "ctx", None),
        P("dp", "ctx", None),
        P("dp", "ctx", None),
        P(("dp", "ctx"), None),
        P("dp", "ctx", None),
    )
    out_specs = (
        P("dp", "ctx", None),
        P("dp", "ctx", None),
        P("dp", "ctx", None),
        P("dp", "ctx", None),
    )
    return jax.shard_map(body, mesh=mesh, in_specs=in_specs, out_specs=out_specs, check_vma=False)
```

profile of v0, /device:TPU:1, one launch (start us, length us, event | category | flops | bytes accessed | tf_op | source)
XLA Modules:
  0.0 575.8 jit_solution(17110521173736781467)
XLA Ops:
  9.3 1.9 copy.35
  11.2 83.5 %all-gather.7.cloned.1.call-done = bf16[4096,2048]{1,0:T(8,128)(2,1)} async-done(((bf16[32,2048]{1,0:T(8,128)(2,1)}), bf16[4096,2048]{1,0:T(8,128)(2,1)}) %all-gather.7.cloned.1.call-update) | async-done | bytes 16777232 | tf_op jit(solution)/shard_map/all_gather | solution.py:110
  94.8 12.6 %convolution_convert_fusion = bf16[128,4096]{1,0:T(8,128)(2,1)} fusion(bf16[4096,2048]{1,0:T(8,128)(2,1)} %all-gather.7.cloned.1.call-done, bf16[1,128,2048]{2,1,0:T(8,128)(2,1)S(1)} %copy-done), kind=kOutput, calls=%fused_computation.43 | convolution fusion | flops 2148007936 | bytes 18350080 | tf_op jit(solution)/shard_map/dot_general | solution.py:112
  107.4 2.7 fusion.31
  114.0 1.9 fusion.34
  116.0 21.5 %all-gather.2 = s32[32,1,64]{2,1,0:T(1,128)S(1)} all-gather(s32[1,1,64]{2,1,0:T(1,128)S(1)} %get-tuple-element.140), channel_id=1, replica_groups=mesh['dp'=4,'ctx'=32] {'ctx'}, dimensions={0}, use_global_device_ids=true | all-gather | bytes 8448 | tf_op jit(solution)/shard_map/all_gather | solution.py:84
  139.7 16.4 %while.25 = (s32[]{:T(128)}, bf16[8,8,128,128]{3,2,1,0:T(8,128)(2,1)}, f32[8,128,8,64]{1,3,2,0:T(8,128)}, f32[128,128]{1,0:T(8,128)S(1)}, s32[8,128,8]{1,2,0:T(8...) while((s32[]{:T(128)}, bf16[8,8,128,128]{3,2,1,0:T(8,128)(2,1)}, f32[8,128,8,64]{1,3,2,0:T(8,128)}, ...), condition=%wide.region_2.3_spmd, body=%wide.region_1.2_spmd.sunk | while | flops 18382848 | bytes 992349 | solution.py:32
  159.0 26.1 %while.26 = (s32[]{:T(128)}, f32[128,128]{1,0:T(8,128)S(1)}, f32[8,128,8,64]{1,3,2,0:T(8,128)}, s32[8,128,8]{1,2,0:T(8,128)S(1)}, bf16[8,128,8,64]{1,3,2,0:T(8,1...) while((s32[]{:T(128)}, f32[128,128]{1,0:T(8,128)S(1)}, ...), condition=%wide.region_6.7_spmd.clone, body=%wide.region_4.6_spmd.clone.sunk | while | flops 34504704 | bytes 1231475 | solution.py:53
  160.3 2.0 fusion.90
  163.5 2.0 fusion.90
  166.8 1.9 fusion.90
  173.2 1.9 fusion.90
  176.5 1.9 fusion.90
  179.7 2.1 fusion.90
  183.1 2.0 fusion.90
  185.4 49.2 %all-gather.11.cloned.1.call-done = bf16[4096,4096]{0,1:T(8,128)(2,1)} async-done(((bf16[128,4096]{0,1:T(8,128)(2,1)}), bf16[4096,4096]{0,1:T(8,128)(2,1)}) %all-gather.11.cloned.1.call-update) | async-done | bytes 33554448 | tf_op jit(solution)/shard_map/all_gather | solution.py:119
  234.5 23.8 %copy.46 = bf16[512,8,32,128]{3,2,1,0:T(8,128)(2,1)} copy(bf16[512,8,32,128]{3,1,2,0:T(8,128)(2,1)} %bitcast.164) | data formatting | bytes 67108864
  258.5 29.8 %fusion.64 = f32[4096,1,128]{2,1,0:T(1,128)S(1)} fusion(f32[32,4096,1]{0,2,1:T(1,128)S(1)} %bitcast.179, bf16[32,128,4096]{1,0,2:T(8,128)(2,1)} %bitcast.165), kind=kOutput, calls=%fused_computation.95 | convolution fusion | flops 201326592 | bytes 36175872 | tf_op jit(solution)/shard_map/ksi,ki->si/dot_general | solution.py:101
  289.9 2.3 copy.36
  292.1 2.3 fusion.40
  294.4 159.6 %all-gather.9.cloned.1.call-done = f32[4096,4096]{0,1:T(8,128)} async-done(((f32[128,4096]{0,1:T(8,128)}), f32[4096,4096]{0,1:T(8,128)}) %all-gather.9.cloned.1.call-update) | async-done | bytes 67108880 | tf_op jit(solution)/shard_map/all_gather | solution.py:104
  454.0 44.1 %copy.45 = f32[512,8,32,128]{3,2,1,0:T(8,128)} copy(f32[512,8,32,128]{3,1,2,0:T(8,128)} %bitcast.60) | data formatting | bytes 134217728
  498.3 58.8 %fusion.63 = f32[4096,1,128]{2,1,0:T(1,128)S(1)} fusion(f32[32,4096,1]{0,2,1:T(1,128)S(1)} %bitcast.170, f32[32,128,4096]{1,0,2:T(8,128)} %bitcast.62), kind=kOutput, calls=%fused_computation.94 | convolution fusion | flops 201326592 | bytes 69730304 | tf_op jit(solution)/shard_map/ksi,ki->si/dot_general | solution.py:101
  558.3 11.0 %fusion.33 = bf16[1,128,2048]{2,1,0:T(8,128)(2,1)} fusion(bf16[4096,2048]{1,0:T(8,128)(2,1)} %all-gather.7.cloned.1.call-done, f32[128,4096]{0,1:T(8,128)} %bitcast.176, f32[128,4096]{0,1:T(8,128)} %bitcast.169, f32[4096,128]{1,0:T(8,128)S(1)} %bitcast.167, bf16[1,128,128]{2,1,0:T(8,128)(2,1)S(1)} %copy-done.10), kind=kOutput, calls=%fused_computation.52 | convolution fusion | flops 2284584960 | bytes 23625728 | tf_op jit(solution)/shard_map/dot_general | solution.py:111
  (132 shorter events, 42.7 us)
Async XLA Ops:
  7.2 87.6 %copy-start = (bf16[1,128,2048]{2,1,0:T(8,128)(2,1)S(1)}, bf16[1,128,2048]{2,1,0:T(8,128)(2,1)}, u32[]{:S(2)}) copy-start(bf16[1,128,2048]{2,1,0:T(8,128)(2,1)} %param.15) | copy-start | bytes 1572868
  7.2 87.6 %all-gather.7.cloned.1.call-start = ((), (), s32[]{:S(2)}) async-start(), calls=%async_computation | async-start | bytes 16908288 | tf_op jit(solution)/shard_map/all_gather | solution.py:110
  7.9 226.6 %all-gather.11.cloned.1.call-start = ((), (), s32[]{:S(2)}) async-start(), calls=%async_computation.2 | async-start | bytes 34603008 | tf_op jit(solution)/shard_map/all_gather | solution.py:119
  9.3 2.0 copy-start.2
  11.2 96.1 %copy-start.10 = (bf16[1,128,128]{2,1,0:T(8,128)(2,1)S(1)}, bf16[1,128,128]{2,1,0:T(8,128)(2,1)}, u32[]{:S(2)}) copy-start(bf16[1,128,128]{2,1,0:T(8,128)(2,1)} %param.12) | copy-start | bytes 98308
  94.8 12.6 %copy-start.3 = (f32[128,4096]{1,0:T(8,128)S(1)}, f32[128,4096]{1,0:T(8,128)}, u32[]{:S(2)}) copy-start(f32[128,4096]{1,0:T(8,128)} %copy.35) | copy-start | bytes 6291460
  110.1 343.9 %all-gather.9.cloned.1.call-start = ((), (), s32[]{:S(2)}) async-start(), calls=%async_computation.1 | async-start | bytes 69206016 | tf_op jit(solution)/shard_map/all_gather | solution.py:104
  110.2 2.0 copy-start.9
  139.7 16.4 %copy-start.5 = (bf16[128,4096]{1,0:T(8,128)(2,1)S(1)}, bf16[128,4096]{1,0:T(8,128)(2,1)}, u32[]{:S(2)}) copy-start(bf16[128,4096]{1,0:T(8,128)(2,1)} %convolution_convert_fusion) | copy-start | bytes 3145732
  258.5 29.8 %copy-start.7 = (f32[128,4096]{0,1:T(8,128)S(1)}, f32[128,4096]{0,1:T(8,128)}, u32[]{:S(2)}) copy-start(f32[128,4096]{0,1:T(8,128)} %get-tuple-element.142) | copy-start | bytes 6291460
  258.5 29.8 %copy-start.8 = (f32[8,128,8,64]{1,3,2,0:T(8,128)S(1)}, f32[8,128,8,64]{1,3,2,0:T(8,128)}, u32[]{:S(2)}) copy-start(f32[8,128,8,64]{1,3,2,0:T(8,128)} %get-tuple-element.77) | copy-start | bytes 6291460
  498.3 58.9 %copy-start.4 = (f32[128,4096]{1,0:T(8,128)S(1)}, f32[128,4096]{1,0:T(8,128)}, u32[]{:S(2)}) copy-start(f32[128,4096]{1,0:T(8,128)} %copy.35) | copy-start | bytes 6291460
  498.3 58.9 %copy-start.6 = (bf16[128,4096]{1,0:T(8,128)(2,1)S(1)}, bf16[128,4096]{1,0:T(8,128)(2,1)}, u32[]{:S(2)}) copy-start(bf16[128,4096]{1,0:T(8,128)(2,1)} %convolution_convert_fusion) | copy-start | bytes 3145732
  558.3 11.0 %copy-start.1 = (bf16[1,128,2048]{2,1,0:T(8,128)(2,1)S(1)}, bf16[1,128,2048]{2,1,0:T(8,128)(2,1)}, u32[]{:S(2)}) copy-start(bf16[1,128,2048]{2,1,0:T(8,128)(2,1)} %param.15) | copy-start | bytes 1572868
Sparse Core Ops, SparseCore 0:
  11.1 83.5 all-gather.6
  110.2 124.2 all-gather.10
  236.7 217.2 all-gather.8
where the time goes:
time: 576 us
  waiting for transfers between devices  293 us (51%)
  matrix products  156 us (27%)
  local copies, waits for them, and re-layouts  80.1 us (14%)
  blocking collectives  21.5 us (4%)
  between operations  14 us (2%)
  other arithmetic  10.4 us (2%)
    all_gather x1, waiting for transfers between devices, body(): lax.all_gather(term[None], 'ctx', axis=0, tiled=True)  160 us
    dot_general x2, matrix products, weighted_add(): jnp.einsum('ksi,ki->si', piece, weight_wide, precision=lax.Precision.HIGH...  88.7 us
    all_gather x1, waiting for transfers between devices, body(): whole_proj = lax.all_gather(w_out, ('dp', 'ctx'), axis=0, tiled=True)  83.5 us
    unnamed x28, local copies, waits for them, and re-layouts  72.1 us
    all_gather x1, waiting for transfers between devices, body(): lax.all_gather(adjoint_term[None].astype(jnp.bfloat16), 'ctx', axis=0, ti...  49.2 us
    all_gather x1, blocking collectives, body(): all_totals = lax.all_gather(totals[None, :], 'ctx', axis=0, tiled=True)  21.5 us
    dot_general x8, matrix products, backward_one_group(): jnp.einsum('gtr,tgp->rgp', mix, d_part, preferred_element_type=jnp.float32)  15.7 us
    dot_general x1, matrix products, body(): lax.dot_general(grad_out, whole_proj, (((1,), (1,)), ((), ())), preferred...  12.6 us
  transfers between devices with their start and end apart: 3, of which 3 were waited for; matrix products, arithmetic and copies ran while one was open for 20% of the time, Pallas kernels for 0%

commit v1 on v0

--- a/solution.py
+++ b/solution.py
@@ -1,9 +1,14 @@
+import functools
+
 import jax
 import jax.numpy as jnp
 from jax import lax
+from jax.experimental import pallas as pl
+from jax.experimental.pallas import tpu as pltpu
 from jax.sharding import PartitionSpec as P
 
 decay_unit = 5e-05
+MESH = pl.DeviceIdType.MESH
 
 
 def causal_decay(local_group):
@@ -56,6 +61,83 @@
         (mixes, x_groups, d_groups, l_groups),
     )
     return (kernel, flows.transpose(1, 0, 2, 3).reshape(rows, inner))
+
+
+def scan_kernel(n, reverse, send, decay, out, recv, recv_decay, stage, sems):
+    me = lax.axis_index("ctx")
+    state = send.shape[1]
+    barrier = pltpu.get_barrier_semaphore()
+
+    def greet(i, carry):
+        pl.semaphore_signal(
+            barrier, inc=1, device_id={"ctx": lax.rem(me + i, n)}, device_id_type=MESH
+        )
+        return carry
+
+    lax.fori_loop(1, n, greet, 0)
+    pl.semaphore_wait(barrier, n - 1)
+
+    def exchange(source, target, first):
+        def copy(source_part, target_part, peer):
+            return pltpu.make_async_remote_copy(
+                src_ref=source_part,
+                dst_ref=target_part,
+                send_sem=sems.at[first],
+                recv_sem=sems.at[first + 1],
+                device_id={"ctx": peer},
+                device_id_type=MESH,
+            )
+
+        def post(i, carry):
+            peer = lax.rem(me + i, n)
+            copy(source.at[peer], target.at[me], peer).start()
+            return carry
+
+        lax.fori_loop(1, n, post, 0)
+        return copy(source.at[pl.ds(0, n - 1)], target.at[pl.ds(0, n - 1)], lax.rem(me + 1, n))
+
+    decays = exchange(decay, recv_decay, 0)
+    terms = exchange(send, recv, 2)
+    recv_decay[me] = decay[me]
+    recv[me] = send[me]
+    decays.wait()
+    terms.wait()
+
+    def step(i, carry):
+        k = n - 1 - i if reverse else i
+        stage[k] = carry.astype(jnp.bfloat16)
+        d = recv_decay[k].astype(jnp.float32)
+        d = d[0:1] + d[1:2] + d[2:3]
+        return d * carry + recv[k].astype(jnp.float32)
+
+    lax.fori_loop(0, n, step, jnp.zeros((state, 128), jnp.float32))
+    result = exchange(stage, out, 4)
+    out[me] = stage[me]
+    result.wait()
+
+
+def block_scan(term, decay_rows, reverse):
+    state, inner = term.shape
+    n = lax.axis_size("ctx")
+    send = term.astype(jnp.bfloat16).reshape(state, n, inner // n).transpose(1, 0, 2)
+    vmem = pl.BlockSpec(memory_space=pltpu.VMEM)
+    out = pl.pallas_call(
+        functools.partial(scan_kernel, n, reverse),
+        out_shape=jax.ShapeDtypeStruct(send.shape, jnp.bfloat16),
+        in_specs=[vmem, vmem],
+        out_specs=vmem,
+        scratch_shapes=[
+            pltpu.VMEM(send.shape, jnp.bfloat16),
+            pltpu.VMEM(decay_rows.shape, jnp.bfloat16),
+            pltpu.VMEM(send.shape, jnp.bfloat16),
+            pltpu.SemaphoreType.DMA((6,)),
+        ],
+        compiler_params=pltpu.CompilerParams(
+            collective_id=1 if reverse else 0, has_side_effects=True
+        ),
+        name="scan_back" if reverse else "scan_forward",
+    )(send, decay_rows)
+    return out.transpose(1, 0, 2).reshape(state, inner)
 
 
 def body(x_in, b_in, c_in, log_decay, w_out, cotangent):
@@ -67,61 +149,38 @@
     rows, inner = x_bf.shape
     heads = steps.shape[1]
     width = inner // heads
-    length = rows * lax.axis_size("ctx")
+    n = lax.axis_size("ctx")
+    length = rows * n
     scale = (b_blk.shape[1] * length) ** (-0.5)
     group = 8
     local = jnp.cumsum(steps, axis=0)
     totals = local[-1]
+    whole_proj = lax.all_gather(w_out, ("dp", "ctx"), axis=0, tiled=True)
     fall_wide = jnp.repeat(jnp.exp(-decay_unit * local.astype(jnp.float32)), width, axis=1)
     tail_wide = jnp.repeat(
         jnp.exp(-decay_unit * (totals[None, :] - local).astype(jnp.float32)), width, axis=1
     )
+    decay = jnp.repeat(jnp.exp(-decay_unit * totals.astype(jnp.float32)), width)
+    high = lax.reduce_precision(decay, 8, 7)
+    middle = lax.reduce_precision(decay - high, 8, 7)
+    low = decay - high - middle
+    decay_rows = jnp.stack([high, middle, low] + [jnp.zeros_like(high)] * 13)
+    decay_rows = decay_rows.astype(jnp.bfloat16).reshape(16, n, inner // n).transpose(1, 0, 2)
     scores = jnp.dot(c_blk, b_blk.T, preferred_element_type=jnp.float32)
-    mixes, y_intra = forward_inside_group(x_bf, local, scores, scale, group, width)
     shifted = (x_bf * tail_wide).astype(jnp.bfloat16)
     term = jnp.dot(b_blk.T, shifted, preferred_element_type=jnp.float32)
-    mine = lax.axis_index("ctx")
-    all_totals = lax.all_gather(totals[None, :], "ctx", axis=0, tiled=True)
-    before_sum = jnp.cumsum(all_totals, axis=0) - all_totals
-    mine_before = lax.dynamic_slice_in_dim(before_sum, mine, 1, 0)
-    mine_total = lax.dynamic_slice_in_dim(all_totals, mine, 1, 0)
-
-    def weighted_add(carry, piece, later):
-        count = piece.shape[0]
-        index_set = jnp.arange(count, dtype=jnp.int32)
-        if later:
-            span = before_sum - mine_before - mine_total
-            live = index_set > mine
-        else:
-            span = mine_before - before_sum - all_totals
-            live = index_set < mine
-        span = jnp.maximum(span, 0).astype(jnp.float32)
-        weight = jnp.where(live[:, None], jnp.exp(-decay_unit * span), jnp.float32(0.0))
-        weight_wide = jnp.repeat(weight, width, axis=1)
-        return carry + jnp.einsum("ksi,ki->si", piece, weight_wide, precision=lax.Precision.HIGHEST)
-
-    before = weighted_add(
-        jnp.zeros_like(term), lax.all_gather(term[None], "ctx", axis=0, tiled=True), False
-    )
-    before_bf = before.astype(jnp.bfloat16)
+    before_bf = block_scan(term, decay_rows, False)
+    mixes, y_intra = forward_inside_group(x_bf, local, scores, scale, group, width)
     mixed = (
         y_intra + scale * fall_wide * jnp.dot(c_blk, before_bf, preferred_element_type=jnp.float32)
     ).astype(jnp.bfloat16)
-    whole_proj = lax.all_gather(w_out, ("dp", "ctx"), axis=0, tiled=True)
     out = jnp.dot(mixed, whole_proj, preferred_element_type=jnp.float32).astype(jnp.bfloat16)
     back_bf = lax.dot_general(
         grad_out, whole_proj, (((1,), (1,)), ((), ())), preferred_element_type=jnp.float32
     ).astype(jnp.bfloat16)
     dshift = (back_bf * fall_wide).astype(jnp.bfloat16)
     adjoint_term = jnp.dot(c_blk.T, dshift, preferred_element_type=jnp.float32)
-    after = weighted_add(
-        jnp.zeros_like(adjoint_term),
-        lax.all_gather(adjoint_term[None].astype(jnp.bfloat16), "ctx", axis=0, tiled=True).astype(
-            jnp.float32
-        ),
-        True,
-    )
-    after_bf = after.astype(jnp.bfloat16)
+    after_bf = block_scan(adjoint_term, decay_rows, True)
     kernel, dx_intra = backward_intra(mixes, x_bf, back_bf, local, scale, group, width)
     kernel_bf = kernel.astype(jnp.bfloat16)
     grad_x = (

time: 576 us -> 230 us (0.40)
  waiting for transfers between devices: 293 us -> 19.5 us
  Pallas kernels: 0 us -> 84.4 us
  matrix products: 156 us -> 75.9 us
  local copies, waits for them, and re-layouts: 80.1 us -> 26.3 us
  blocking collectives: 21.5 us -> 0 us
    all_gather x2 -> x0, waiting for transfers between devices: 209 us -> none  [the longest x1 160 us: body(): lax.all_gather(term[None], 'ctx', axis=0, tiled=True)]
    dot_general x2 -> x0, matrix products: 88.7 us -> none  [weighted_add(): jnp.einsum('ksi,ki->si', piece, weight_wide, precision=lax.Precision.HIGH...]
    pallas_call x0 -> x2, Pallas kernels: none -> 84.4 us  [block_scan(): pl.pallas_call(functools.partial(scan_kernel, n, reverse), out_shape=jax....]
    unnamed x28 -> x18, local copies, waits for them, and re-layouts: 72.1 us -> 5.97 us
    all_gather x1, waiting for transfers between devices: 83.5 us -> 18.8 us  [body(): whole_proj = lax.all_gather(w_out, ('dp', 'ctx'), axis=0, tiled=True)]
    all_gather x1 -> x0, blocking collectives: 21.5 us -> none  [body(): all_totals = lax.all_gather(totals[None, :], 'ctx', axis=0, tiled=True)]
    dot_general x8, matrix products: 8.72 us -> 15.9 us  [forward_one_group(): jnp.einsum('gtr,rgp->tgp', mix, x_part, preferred_element_type=jnp.float32)]
  transfers between devices with their start and end apart: 3 -> 1, of which waited for: 3 -> 1; matrix products, arithmetic and copies ran while one was open for 20% -> 17% of each run, Pallas kernels for 0% -> 20%
where the time goes in v1:
time: 230 us; the launch traced here: 229 us
  Pallas kernels  84.4 us (37%)
  matrix products  75.9 us (33%)
  local copies, waits for them, and re-layouts  26.3 us (11%)
  waiting for transfers between devices  19.5 us (8%)
  between operations  14.2 us (6%)
  other arithmetic  8.45 us (4%)
    pallas_call x2, Pallas kernels, block_scan(): pl.pallas_call(functools.partial(scan_kernel, n, reverse), out_shape=jax....  84.4 us
    all_gather x1, waiting for transfers between devices, body(): whole_proj = lax.all_gather(w_out, ('dp', 'ctx'), axis=0, tiled=True)  18.8 us
    dot_general x8, matrix products, forward_one_group(): jnp.einsum('gtr,rgp->tgp', mix, x_part, preferred_element_type=jnp.float32)  15.9 us
    dot_general x8, matrix products, backward_one_group(): jnp.einsum('gtr,tgp->rgp', mix, d_part, preferred_element_type=jnp.float32)  15.5 us
    dot_general x1, matrix products, body(): lax.dot_general(grad_out, whole_proj, (((1,), (1,)), ((), ())), preferred...  12.4 us
    dot_general x1, matrix products, body(): jnp.dot(mixed, whole_proj, preferred_element_type=jnp.float32)  11.2 us
    dot_general x8, matrix products, backward_one_group(): jnp.einsum('tgp,rgp->gtr', d_part, x_part, preferred_element_type=jnp.flo...  10.5 us
    dynamic_update_slice x8, other arithmetic, forward_inside_group(): lax.scan(forward_one_group, jnp.zeros((), jnp.float32), (x_groups, l_grou...  7.4 us
  transfers between devices with their start and end apart: 1, of which 1 were waited for; matrix products, arithmetic and copies ran while one was open for 17% of the time, Pallas kernels for 20%

profile of v1, /device:TPU:1, one launch (start us, length us, event | category | flops | bytes accessed | tf_op | source)
XLA Modules:
  0.0 229.1 jit_solution(709756144832819739)
XLA Ops:
  15.7 44.8 %scan_forward.1 = bf16[32,128,128]{2,1,0:T(8,128)(2,1)} custom-call(bf16[32,128,128]{2,1,0:T(8,128)(2,1)} %bitcast.159, bf16[32,16,128]{2,1,0:T(8,128)(2,1)} %bitcast.166), custom_call_target="tpu_custom_call" | custom-call | tf_op jit(solution)/shard_map/scan_forward/pallas_call | solution.py:124
  60.5 2.4 %copy.38 = bf16[128,32,128]{0,2,1:T(8,128)(2,1)} copy(bf16[128,32,128]{2,0,1:T(8,128)(2,1)} %bitcast.162) | data formatting | bytes 2097152 | tf_op jit(solution)/shard_map/transpose | solution.py:140
  68.3 23.6 %while.25 = (s32[]{:T(128)}, bf16[8,8,128,128]{3,2,1,0:T(8,128)(2,1)}, f32[8,128,8,64]{1,3,2,0:T(8,128)}, f32[128,128]{1,0:T(8,128)S(1)}, s32[8,128,8]{1,2,0:T(8...) while((s32[]{:T(128)}, bf16[8,8,128,128]{3,2,1,0:T(8,128)(2,1)}, f32[8,128,8,64]{1,3,2,0:T(8,128)}, ...), condition=%wide.region_2.3_spmd, body=%wide.region_1.2_spmd.sunk | while | flops 18382848 | bytes 992349 | solution.py:37
  69.3 2.0 fusion.77
  72.2 2.0 fusion.77
  75.2 2.0 fusion.77
  78.1 2.0 fusion.77
  81.1 2.0 fusion.77
  84.0 2.0 fusion.77
  86.9 2.0 fusion.77
  89.9 2.0 fusion.77
  91.9 18.8 %all-gather.2.cloned.1.call-done = bf16[4096,2048]{1,0:T(8,128)(2,1)} async-done(((bf16[32,2048]{1,0:T(8,128)(2,1)}), bf16[4096,2048]{1,0:T(8,128)(2,1)}) %all-gather.2.cloned.1.call-update) | async-done | bytes 16777232 | tf_op jit(solution)/shard_map/all_gather | solution.py:158
  110.7 12.4 %convolution_convert_fusion = bf16[128,4096]{1,0:T(8,128)(2,1)} fusion(bf16[4096,2048]{1,0:T(8,128)(2,1)} %all-gather.2.cloned.1.call-done, bf16[1,128,2048]{2,1,0:T(8,128)(2,1)S(1)} %copy-done), kind=kOutput, calls=%fused_computation.42 | convolution fusion | flops 2148007936 | bytes 18350080 | tf_op jit(solution)/shard_map/dot_general | solution.py:178
  123.0 2.3 copy.39
  126.9 26.5 %while.26 = (s32[]{:T(128)}, f32[128,128]{1,0:T(8,128)S(1)}, f32[8,128,8,64]{1,3,2,0:T(8,128)}, s32[8,128,8]{1,2,0:T(8,128)S(1)}, bf16[8,128,8,64]{1,3,2,0:T(8,1...) while((s32[]{:T(128)}, f32[128,128]{1,0:T(8,128)S(1)}, ...), condition=%wide.region_5.6_spmd.clone, body=%wide.region_3.5_spmd.clone.sunk | while | flops 34504704 | bytes 1231475 | solution.py:58
  151.4 2.0 fusion.83
  153.7 2.7 %convolution_convert_fusion.1 = bf16[4096,128]{1,0:T(8,128)(2,1)} fusion(bf16[1,128,128]{2,1,0:T(8,128)(2,1)S(1)} %copy-done.7, f32[128,4096]{1,0:T(8,128)S(1)} %copy.41, bf16[128,4096]{1,0:T(8,128)(2,1)} %convolution_convert_fusion), kind=kOutput, calls=%fused_computation.45 | convolution fusion | flops 136314880 | bytes 4227072 | tf_op jit(solution)/shard_map/dot_general | solution.py:182
  156.4 2.3 copy.42
  158.7 39.6 %scan_back.1 = bf16[32,128,128]{2,1,0:T(8,128)(2,1)} custom-call(bf16[32,128,128]{2,1,0:T(8,128)(2,1)} %bitcast.160, bf16[32,16,128]{2,1,0:T(8,128)(2,1)} %bitcast.167), custom_call_target="tpu_custom_call" | custom-call | tf_op jit(solution)/shard_map/scan_back/pallas_call | solution.py:124
  198.3 2.3 copy.43
  201.8 3.1 %fusion.31 = bf16[1,128,4096]{1,2,0:T(8,128)(2,1)} fusion(f32[128,4096]{0,1:T(8,128)} %bitcast.154, f32[128,4096]{0,1:T(8,128)S(1)} %bitcast.155, bf16[128,4096]{0,1:T(8,128)(2,1)S(1)} %bitcast.153, bf16[1,128,128]{2,1,0:T(8,128)(2,1)S(1)} %copy-done.6), kind=kOutput, calls=%fused_computation.47 | convolution fusion | flops 135790592 | bytes 6324224 | tf_op jit(solution)/shard_map/dot_general | solution.py:187
  204.9 2.3 copy.44
  207.2 2.8 %fusion.39 = bf16[1,128,128]{2,1,0:T(8,128)(2,1)} fusion(f32[128,128]{1,0:T(8,128)S(1)} %fusion.48, bf16[128,4096]{0,1:T(8,128)(2,1)} %bitcast.149, bf16[128,4096]{0,1:T(8,128)(2,1)} %bitcast.152), kind=kOutput, calls=%fused_computation.60 | convolution fusion | flops 134266880 | bytes 2195456 | tf_op jit(solution)/shard_map/dot_general | solution.py:191
  211.0 11.2 %fusion.32 = bf16[1,128,2048]{2,1,0:T(8,128)(2,1)} fusion(bf16[4096,2048]{1,0:T(8,128)(2,1)} %all-gather.2.cloned.1.call-done, f32[128,4096]{0,1:T(8,128)} %bitcast.156, bf16[128,4096]{0,1:T(8,128)(2,1)} %bitcast.150, f32[128,4096]{0,1:T(8,128)} %bitcast.147, bf16[1,128,128]{2,1,0:T(8,128)(2,1)S(1)} %copy-done.7), kind=kOutput, calls=%fused_computation.49 | convolution fusion | flops 2284060672 | bytes 22577152 | tf_op jit(solution)/shard_map/dot_general | solution.py:177
  (121 shorter events, 49.8 us)
Async XLA Ops:
  7.2 103.5 %copy-start = (bf16[1,128,2048]{2,1,0:T(8,128)(2,1)S(1)}, bf16[1,128,2048]{2,1,0:T(8,128)(2,1)}, u32[]{:S(2)}) copy-start(bf16[1,128,2048]{2,1,0:T(8,128)(2,1)} %param.15) | copy-start | bytes 1572868
  7.2 103.5 %all-gather.2.cloned.1.call-start = ((), (), s32[]{:S(2)}) async-start(), calls=%async_computation | async-start | bytes 16908288 | tf_op jit(solution)/shard_map/all_gather | solution.py:158
  9.0 3.1 %copy-start.6 = (bf16[1,128,128]{2,1,0:T(8,128)(2,1)S(1)}, bf16[1,128,128]{2,1,0:T(8,128)(2,1)}, u32[]{:S(2)}) copy-start(bf16[1,128,128]{2,1,0:T(8,128)(2,1)} %param.11) | copy-start | bytes 98308
  10.7 1.9 copy-start.5
  11.1 1.0 copy-start.2
  64.6 2.0 copy-start.7
  200.5 1.2 copy-start.4
  207.2 2.8 %copy-start.1 = (bf16[128,4096]{1,0:T(8,128)(2,1)S(1)}, bf16[128,4096]{1,0:T(8,128)(2,1)}, u32[]{:S(2)}) copy-start(bf16[128,4096]{1,0:T(8,128)(2,1)} %convolution_convert_fusion) | copy-start | bytes 3145732
  207.2 2.8 %copy-start.3 = (bf16[128,32,128]{0,2,1:T(8,128)(2,1)S(1)}, bf16[128,32,128]{0,2,1:T(8,128)(2,1)}, u32[]{:S(2)}) copy-start(bf16[128,32,128]{0,2,1:T(8,128)(2,1)} %copy.38) | copy-start | bytes 3145732
Sparse Core Ops, SparseCore 0:
  11.1 99.4 all-gather.1

commit v2 on v0

v2 whole, which is shorter than its diff:
```python
import functools

import jax
import jax.numpy as jnp
from jax import lax
from jax.experimental import pallas as pl
from jax.experimental.pallas import tpu as pltpu
from jax.sharding import PartitionSpec as P

decay_unit = 5e-05
rate = decay_unit * 1.4426950408889634
MESH = pl.DeviceIdType.MESH
F32 = jnp.float32
BF = jnp.bfloat16
LANES = 128


def dot(a, b):
    return lax.dot_general(a, b, (((1,), (0,)), ((), ())), preferred_element_type=F32)


def dot_nt(a, b):
    return lax.dot_general(a, b, (((1,), (1,)), ((), ())), preferred_element_type=F32)


def flip(a):
    return a.astype(F32).T


def span(j, size=LANES):
    return pl.ds(pl.multiple_of(j * size, size), size)


def grid_of(rows, columns):
    return (
        lax.broadcasted_iota(jnp.int32, (rows, columns), 0),
        lax.broadcasted_iota(jnp.int32, (rows, columns), 1),
    )


def greet_all(n):
    me = lax.axis_index("ctx")
    barrier = pltpu.get_barrier_semaphore()

    def greet(i, carry):
        pl.semaphore_signal(
            barrier, inc=1, device_id={"ctx": lax.rem(me + i, n)}, device_id_type=MESH
        )
        return carry

    lax.fori_loop(1, n, greet, 0)
    return barrier


def copy_to(peer, source, target, sems, first):
    return pltpu.make_async_remote_copy(
        src_ref=source,
        dst_ref=target,
        send_sem=sems.at[first],
        recv_sem=sems.at[first + 1],
        device_id={"ctx": peer},
        device_id_type=MESH,
    )


def finish(n, source, target, sems, first):
    peer = lax.rem(lax.axis_index("ctx") + 1, n)
    some = pl.ds(0, n - 1)
    copy_to(peer, source.at[some], target.at[some], sems, first).wait()


def accumulate_decay(steps, level):
    rows, heads = steps.shape
    row, column = grid_of(rows, rows)
    ones = jnp.where(row >= column, 1.0, 0.0).astype(BF)
    value = steps[...]
    high = (value >> 7).astype(F32).astype(BF)
    low = (value & 127).astype(F32).astype(BF)
    level[...] = jnp.zeros_like(level)
    level[:, :heads] = (dot(ones, high) * 128.0 + dot(ones, low)) * rate


def columns_of(level, j):
    rolled = pltpu.roll(level[...], lax.rem(LANES - 2 * j, LANES), 1)
    shape = rolled.shape
    return jnp.broadcast_to(rolled[:, 0:1], shape), jnp.broadcast_to(rolled[:, 1:2], shape)


def paired(level, j):
    one, two = columns_of(level, j)
    _, column = grid_of(*one.shape)
    both = jnp.where(column < LANES // 2, one, two)
    return both, both[both.shape[0] - 1 :]


def split_heads(value):
    _, column = grid_of(*value.shape)
    wide = value.astype(F32)
    left = jnp.where(column < LANES // 2, wide, 0.0).astype(BF)
    right = jnp.where(column < LANES // 2, 0.0, wide).astype(BF)
    return jnp.concatenate([left, right], axis=0)


def forward_kernel(
    n, scale, x, b, c, steps, mixed, before, level, decays, level_t, masked, b_t, y, send, recv,
    stage, sems,
):
    me = lax.axis_index("ctx")
    rows = x.shape[0]
    state = b.shape[1]
    barrier = greet_all(n)
    accumulate_decay(steps, level)
    level_t[...] = flip(level[...])
    row, column = grid_of(rows, rows)
    masked[...] = jnp.where(row >= column, scale * dot_nt(c[...], b[...]), 0.0)
    b_t[...] = flip(b[...]).astype(BF)
    pl.semaphore_wait(barrier, n - 1)

    def send_term(i, carry):
        j = lax.rem(me + i, n)
        both, last = paired(level, j)
        shifted = (x[:, span(j)].astype(F32) * jnp.exp2(both - last)).astype(BF)
        send[j, :state] = dot(b_t[...], shifted).astype(BF)
        d = jnp.exp2(-last)
        high = d.astype(BF).astype(F32)
        middle = (d - high).astype(BF).astype(F32)
        low = d - high - middle
        which, _ = grid_of(16, LANES)
        parts = jnp.where(which == 0, high, jnp.where(which == 1, middle, low))
        send[j, state:] = jnp.where(which < 3, parts, 0.0).astype(BF)

        @pl.when(i < n)
        def _():
            copy_to(j, send.at[j], recv.at[me], sems, 0).start()

        return carry

    lax.fori_loop(1, n + 1, send_term, 0)

    def inside(j, carry):
        one, two = columns_of(level, j)
        first = jnp.exp2(jnp.minimum(level_t[pl.ds(2 * j, 1), :] - one, 0.0))
        second = jnp.exp2(jnp.minimum(level_t[pl.ds(2 * j + 1, 1), :] - two, 0.0))
        mix = jnp.concatenate(
            [(masked[...] * first).astype(BF), (masked[...] * second).astype(BF)], axis=1
        )
        y[j] = dot(mix, split_heads(x[:, span(j)]))
        return carry

    lax.fori_loop(0, n // 2, inside, 0)
    recv[me] = send[me]
    finish(n, send, recv, sems, 0)

    def step(k, carry):
        stage[k] = carry.astype(BF)
        parts = recv[k, state:].astype(F32)
        d = parts[0:1] + parts[1:2] + parts[2:3]
        decays[k] = jnp.broadcast_to(d, (8, LANES))

        @pl.when(k != me)
        def _():
            copy_to(k, stage.at[k], before.at[me], sems, 2).start()

        return d * carry + recv[k, :state].astype(F32)

    lax.fori_loop(0, n, step, jnp.zeros((state, LANES), F32))
    before[me] = stage[me]
    lax.fori_loop(n // 2, n, inside, 0)
    finish(n, stage, before, sems, 2)

    def join(j, carry):
        both, _ = paired(level, j)
        carried = scale * jnp.exp2(-both) * dot(c[...], before[j])
        mixed[:, span(j)] = (y[j] + carried).astype(BF)
        return carry

    lax.fori_loop(0, n, join, 0)


def backward_kernel(
    n, scale, x, b, c, cot, mixed, before, level, decays, w, out, grad_x, grad_b, grad_c,
    level_t, masked_t, c_t, whole, back, dshift, flow, inner_sum, b_sum, c_sum, send, recv, stage,
    after, sems, w_sems,
):
    me = lax.axis_index("ctx")
    rows = x.shape[0]
    state = b.shape[1]
    chunks = w_sems.shape[0]
    depth = w.shape[0] // chunks
    each = n // chunks

    def place(i):
        return lax.rem(me // each + 1 + i, chunks)

    def fetch(i):
        part = span(place(i), depth)
        return pltpu.make_async_copy(w.at[part], whole.at[part], w_sems.at[i])

    def fetch_one(i, carry):
        fetch(i).start()
        return carry

    lax.fori_loop(0, chunks, fetch_one, 0)
    barrier = greet_all(n)
    level_t[...] = flip(level[...])
    row, column = grid_of(rows, rows)
    masked_t[...] = jnp.where(row <= column, scale * dot_nt(b[...], c[...]), 0.0)
    c_t[...] = flip(c[...]).astype(BF)
    inner_sum[...] = jnp.zeros_like(inner_sum)
    b_sum[...] = jnp.zeros_like(b_sum)
    c_sum[...] = jnp.zeros_like(c_sum)
    pl.semaphore_wait(barrier, n - 1)

    def send_term(i, carry):
        fetch(i).wait()
        q = place(i)
        part = dot_nt(cot[...], whole[span(q, depth), :]).astype(BF)
        back[:, span(q, depth)] = part
        for u in range(each):
            j = q * each + u
            both, _ = paired(level, j)
            piece = part[:, u * LANES : (u + 1) * LANES].astype(F32)
            shift = (piece * jnp.exp2(-both)).astype(BF)
            dshift[:, span(j)] = shift
            send[j] = dot(c_t[...], shift).astype(BF)

            @pl.when(j != me)
            def _():
                copy_to(j, send.at[j], recv.at[me], sems, 0).start()

        return carry

    lax.fori_loop(0, chunks, send_term, 0)

    def inside(j, carry):
        one, two = columns_of(level, j)
        first = jnp.exp2(jnp.minimum(one - level_t[pl.ds(2 * j, 1), :], 0.0))
        second = jnp.exp2(jnp.minimum(two - level_t[pl.ds(2 * j + 1, 1), :], 0.0))
        mix = jnp.concatenate(
            [(masked_t[...] * first).astype(BF), (masked_t[...] * second).astype(BF)], axis=1
        )
        part = back[:, span(j)]
        flow[j] = dot(mix, split_heads(part))
        pair = dot_nt(split_heads(x[:, span(j)]), part)
        inner_sum[...] += first * pair[:rows] + second * pair[rows:]
        c_sum[...] += dot_nt(dshift[:, span(j)], before[j])
        return carry

    lax.fori_loop(0, n, inside, 0)
    recv[me] = send[me]
    finish(n, send, recv, sems, 0)

    def step(i, carry):
        k = n - 1 - i
        stage[k] = carry.astype(BF)

        @pl.when(k != me)
        def _():
            copy_to(k, stage.at[k], after.at[me], sems, 2).start()

        return decays[k, 0:1] * carry + recv[k].astype(F32)

    lax.fori_loop(0, n, step, jnp.zeros((state, LANES), F32))
    after[me] = stage[me]

    def project(i, carry):
        out[:, span(i, 256)] = dot(mixed[...], whole[:, span(i, 256)]).astype(BF)
        return carry

    lax.fori_loop(0, out.shape[1] // 256, project, 0)
    kernel_t = jnp.where(row <= column, scale * inner_sum[...], 0.0)
    kernel = kernel_t.T.astype(BF)
    grad_c[...] = (dot(kernel, b[...]) + scale * c_sum[...]).astype(BF)
    finish(n, stage, after, sems, 2)

    def join(j, carry):
        both, last = paired(level, j)
        tail = jnp.exp2(both - last)
        grad_x[:, span(j)] = (flow[j] + scale * tail * dot(b[...], after[j])).astype(BF)
        shifted = (x[:, span(j)].astype(F32) * tail).astype(BF)
        b_sum[...] += dot_nt(shifted, after[j])
        return carry

    lax.fori_loop(0, n, join, 0)
    grad_b[...] = (dot(kernel_t.astype(BF), c[...]) + scale * b_sum[...]).astype(BF)


def body(x_in, b_in, c_in, log_decay, w_out, cotangent):
    x, b, c, steps, cot = x_in[0], b_in[0], c_in[0], log_decay[0], cotangent[0]
    rows, inner = x.shape
    state = b.shape[1]
    n = lax.axis_size("ctx")
    scale = (state * rows * n) ** (-0.5)
    vmem = pl.BlockSpec(memory_space=pltpu.VMEM)
    hbm = pl.BlockSpec(memory_space=pl.ANY)
    shape = jax.ShapeDtypeStruct
    square = pltpu.VMEM((rows, rows), F32)
    blocks = (n, state, LANES)
    whole = lax.all_gather(w_out, ("dp", "ctx"), axis=0, tiled=True)
    mixed, before, level, decays = pl.pallas_call(
        functools.partial(forward_kernel, n, scale),
        out_shape=(
            shape(x.shape, BF), shape(blocks, BF), shape((rows, LANES), F32),
            shape((n, 8, LANES), F32),
        ),
        in_specs=[vmem] * 4,
        out_specs=(vmem,) * 4,
        scratch_shapes=[
            square,
            square,
            pltpu.VMEM((state, rows), BF),
            pltpu.VMEM((n, rows, LANES), F32),
            pltpu.VMEM((n, state + 16, LANES), BF),
            pltpu.VMEM((n, state + 16, LANES), BF),
            pltpu.VMEM(blocks, BF),
            pltpu.SemaphoreType.DMA((4,)),
        ],
        compiler_params=pltpu.CompilerParams(collective_id=0, has_side_effects=True),
        cost_estimate=pl.CostEstimate(
            flops=2000000000, bytes_accessed=8000000, transcendentals=2000000
        ),
        name="forward",
    )(x, b, c, steps)
    chunks = n // 2
    results = pl.pallas_call(
        functools.partial(backward_kernel, n, scale),
        out_shape=(
            shape(cot.shape, BF), shape(x.shape, BF), shape(b.shape, BF), shape(c.shape, BF),
        ),
        in_specs=[vmem] * 8 + [hbm],
        out_specs=(vmem,) * 4,
        scratch_shapes=[
            square,
            square,
            pltpu.VMEM((state, rows), BF),
            pltpu.VMEM(whole.shape, BF),
            pltpu.VMEM(x.shape, BF),
            pltpu.VMEM(x.shape, BF),
            pltpu.VMEM((n, rows, LANES), F32),
            square,
            pltpu.VMEM((rows, state), F32),
            pltpu.VMEM((rows, state), F32),
            pltpu.VMEM(blocks, BF),
            pltpu.VMEM(blocks, BF),
            pltpu.VMEM(blocks, BF),
            pltpu.VMEM(blocks, BF),
            pltpu.SemaphoreType.DMA((4,)),
            pltpu.SemaphoreType.DMA((chunks,)),
        ],
        compiler_params=pltpu.CompilerParams(
            collective_id=1, has_side_effects=True, vmem_limit_bytes=56 * 1024 * 1024
        ),
        name="backward",
    )(x, b, c, cot, mixed, before, level, decays, whole)
    return tuple(r[None] for r in results)


def solution(mesh):
    tokens = P("dp", "ctx", None)
    return jax.shard_map(
        body,
        mesh=mesh,
        in_specs=(tokens, tokens, tokens, tokens, P(("dp", "ctx"), None), tokens),
        out_specs=(tokens, tokens, tokens, tokens),
        check_vma=False,
    )
```

time: 576 us -> 186 us (0.32)
  waiting for transfers between devices: 293 us -> 50.6 us
  matrix products: 156 us -> 0 us
  Pallas kernels: 0 us -> 112 us
  local copies, waits for them, and re-layouts: 80.1 us -> 8.4 us
  blocking collectives: 21.5 us -> 0 us
  other arithmetic: 10.4 us -> 0 us
    all_gather x3 -> x1, waiting for transfers between devices: 292 us -> 49.9 us  [body(): whole = lax.all_gather(w_out, ('dp', 'ctx'), axis=0, tiled=True)]
    dot_general x36 -> x0, matrix products: 156 us -> none  [the longest x2 88.7 us: weighted_add(): jnp.einsum('ksi,ki->si', piece, weight_wide, precision=lax.Precision.HIGH...]
    pallas_call x0 -> x2, Pallas kernels: none -> 112 us  [the longest x1 61.7 us: body(): pl.pallas_call(functools.partial(backward_kernel, n, scale), out_shape=(s...]
    unnamed x28 -> x5, local copies, waits for them, and re-layouts: 72.1 us -> 8.4 us
    all_gather x1 -> x0, blocking collectives: 21.5 us -> none  [body(): all_totals = lax.all_gather(totals[None, :], 'ctx', axis=0, tiled=True)]
    dynamic_update_slice x8 -> x0, other arithmetic: 7.36 us -> none  [forward_inside_group(): lax.scan(forward_one_group, jnp.zeros((), jnp.float32), (x_groups, l_grou...]
  transfers between devices with their start and end apart: 3 -> 1, of which waited for: 3 -> 1; matrix products, arithmetic and copies ran while one was open for 20% -> 1% of each run, Pallas kernels for 0% -> 27%
where the time goes in v2:
time: 186 us; the launch traced here: 185 us
  Pallas kernels  112 us (60%)
  waiting for transfers between devices  50.6 us (27%)
  between operations  14 us (8%)
  local copies, waits for them, and re-layouts  8.4 us (5%)
    pallas_call x1, Pallas kernels, body(): pl.pallas_call(functools.partial(backward_kernel, n, scale), out_shape=(s...  61.7 us
    pallas_call x1, Pallas kernels, body(): pl.pallas_call(functools.partial(forward_kernel, n, scale), out_shape=(sh...  50.3 us
    all_gather x1, waiting for transfers between devices, body(): whole = lax.all_gather(w_out, ('dp', 'ctx'), axis=0, tiled=True)  49.9 us
    unnamed x5, local copies, waits for them, and re-layouts  8.4 us
  transfers between devices with their start and end apart: 1, of which 1 were waited for; matrix products, arithmetic and copies ran while one was open for 1% of the time, Pallas kernels for 27%

profile of v2, /device:TPU:1, one launch (start us, length us, event | category | flops | bytes accessed | tf_op | source)
XLA Modules:
  0.0 185.1 jit_solution(10476724618982578306)
XLA Ops:
  7.2 0.0 all-gather.2.cloned.1.call-start
  7.2 0.7 all-gather.2.cloned.1.call-update
  7.9 1.5 copy.10
  9.4 50.3 %forward.1 = (bf16[128,4096]{1,0:T(8,128)(2,1)}, bf16[32,128,128]{2,1,0:T(8,128)(2,1)}, f32[128,128]{1,0:T(8,128)}, f32[32,8,128]{2,1,0:T(8,128)}) custom-call(bf16[128,4096]{1,0:T(8,128)(2,1)} %bitcast.9, bf16[128,128]{1,0:T(8,128)(2,1)} %bitcast.15, bf16[128,128]{1,0:T(8,128)(2,1)} %bitcast.17, s32[128,64]{1,0:T(8,128)} %bitcast.14), custom_call_target="tpu_custom_call" | custom-call | flops 2000000000 | bytes 8000000 | tf_op jit(solution)/shard_map/forward/pallas_call | solution.py:300
  59.7 49.9 %all-gather.2.cloned.1.call-done.w = bf16[4096,2048]{1,0:T(8,128)(2,1)} async-done(((bf16[32,2048]{1,0:T(8,128)(2,1)}), bf16[4096,2048]{1,0:T(8,128)(2,1)}) %all-gather.2.cloned.1.call-update) | async-done | bytes 16777232 | tf_op jit(solution)/shard_map/all_gather | solution.py:299
  109.6 61.7 %backward.1 = (bf16[128,2048]{1,0:T(8,128)(2,1)}, bf16[128,4096]{1,0:T(8,128)(2,1)}, bf16[128,128]{1,0:T(8,128)(2,1)}, bf16[128,128]{1,0:T(8,128)(2,1)}) custom-call(bf16[128,4096]{1,0:T(8,128)(2,1)} %bitcast.10, bf16[128,128]{1,0:T(8,128)(2,1)} %bitcast.16, bf16[128,128]{1,0:T(8,128)(2,1)} %bitcast.18, bf16[128,2048]{1,0:T(8,128)(2,1)} %bitcast.12, ...), custom_call_target="tpu_custom_call" | custom-call | tf_op jit(solution)/shard_map/backward/pallas_call | solution.py:325
  171.3 1.9 %copy.15 = bf16[1,128,2048]{2,1,0:T(8,128)(2,1)} copy(bf16[1,128,2048]{2,1,0:T(8,128)(2,1)} %bitcast.13) | data formatting | bytes 1048576
  173.2 2.3 %copy.16 = bf16[1,128,4096]{2,1,0:T(8,128)(2,1)} copy(bf16[1,128,4096]{2,1,0:T(8,128)(2,1)} %bitcast.11) | data formatting | bytes 2097152
  175.5 1.4 copy.17
  176.8 1.4 copy.18
Async XLA Ops:
  7.2 102.4 %all-gather.2.cloned.1.call-start = ((), (), s32[]{:S(2)}) async-start(), calls=%async_computation | async-start | bytes 16908288 | tf_op jit(solution)/shard_map/all_gather | solution.py:299
Sparse Core Ops, SparseCore 0:
  11.1 98.4 all-gather.1

commit v3 on v2

v3 whole, which is shorter than its diff:
```python
import functools

import jax
import jax.numpy as jnp
from jax import lax
from jax.experimental import pallas as pl
from jax.experimental.pallas import tpu as pltpu
from jax.sharding import PartitionSpec as P

decay_unit = 5e-05
rate = decay_unit * 1.4426950408889634
MESH = pl.DeviceIdType.MESH
F32 = jnp.float32
BF = jnp.bfloat16
LANES = 128
SIDE = 4
ORDERS = ((1, 0, 2), (0, 2, 1), (2, 1, 0))
CUTS = (0, 640, 1280, 2048)


def dot(a, b):
    return lax.dot_general(a, b, (((1,), (0,)), ((), ())), preferred_element_type=F32)


def dot_nt(a, b):
    return lax.dot_general(a, b, (((1,), (1,)), ((), ())), preferred_element_type=F32)


def flip(a):
    return a.astype(F32).T


def span(j, size=LANES):
    return pl.ds(pl.multiple_of(j * size, size), size)


def grid_of(rows, columns):
    return (
        lax.broadcasted_iota(jnp.int32, (rows, columns), 0),
        lax.broadcasted_iota(jnp.int32, (rows, columns), 1),
    )


def greet_all(n):
    me, seq = lax.axis_index("ctx"), lax.axis_index("dp")
    barrier = pltpu.get_barrier_semaphore()

    def greet(i, carry):
        pl.semaphore_signal(
            barrier, inc=1, device_id={"ctx": lax.rem(me + i, n)}, device_id_type=MESH
        )
        return carry

    lax.fori_loop(1, n, greet, 0)
    for turn in (1, SIDE - 1):
        pl.semaphore_signal(
            barrier, inc=1, device_id={"dp": lax.rem(seq + turn, SIDE)}, device_id_type=MESH
        )
    return barrier


def copy_to(peer, source, target, sems, first):
    return pltpu.make_async_remote_copy(
        src_ref=source,
        dst_ref=target,
        send_sem=sems.at[first],
        recv_sem=sems.at[first + 1],
        device_id={"ctx": peer},
        device_id_type=MESH,
    )


def finish(n, source, target, sems, first):
    peer = lax.rem(lax.axis_index("ctx") + 1, n)
    some = pl.ds(0, n - 1)
    copy_to(peer, source.at[some], target.at[some], sems, first).wait()


def accumulate_decay(steps, level):
    rows, heads = steps.shape
    row, column = grid_of(rows, rows)
    ones = jnp.where(row >= column, 1.0, 0.0).astype(BF)
    value = steps[...]
    high = (value >> 7).astype(F32).astype(BF)
    low = (value & 127).astype(F32).astype(BF)
    level[...] = jnp.zeros_like(level)
    level[:, :heads] = (dot(ones, high) * 128.0 + dot(ones, low)) * rate


def columns_of(level, j):
    rolled = pltpu.roll(level[...], lax.rem(LANES - 2 * j, LANES), 1)
    shape = rolled.shape
    return jnp.broadcast_to(rolled[:, 0:1], shape), jnp.broadcast_to(rolled[:, 1:2], shape)


def paired(level, j):
    one, two = columns_of(level, j)
    _, column = grid_of(*one.shape)
    both = jnp.where(column < LANES // 2, one, two)
    return both, both[both.shape[0] - 1 :]


def split_heads(value):
    _, column = grid_of(*value.shape)
    wide = value.astype(F32)
    left = jnp.where(column < LANES // 2, wide, 0.0).astype(BF)
    right = jnp.where(column < LANES // 2, 0.0, wide).astype(BF)
    return jnp.concatenate([left, right], axis=0)


class Gather:
    def __init__(self, shard, whole, own_sem, ring_send, ring_recv, pair_send, pair_recv):
        ctx = lax.axis_index("ctx")
        self.at = (lax.axis_index("dp"), ctx // (2 * SIDE), lax.rem(ctx // 2, SIDE))
        self.core = lax.rem(ctx, 2)
        self.shard, self.whole = shard, whole
        self.own_sem = own_sem
        self.ring_send, self.ring_recv = ring_send, ring_recv
        self.pair_send, self.pair_recv = pair_send, pair_recv

    def device(self, dim, place, core):
        y, x, z = [place if d == dim else v for d, v in enumerate(self.at)]
        return {"dp": y, "ctx": (x * SIDE + z) * 2 + core}

    def region(self, part, phase, place, rows):
        order = ORDERS[part]
        index = list(self.at)
        for dim in order[:phase]:
            index[dim] = slice(None)
        index[order[phase]] = place
        columns = pl.ds(CUTS[part], CUTS[part + 1] - CUTS[part])
        return self.whole.at[(*index, self.core, rows, columns)]

    def ring(self, part, phase, step):
        dim = ORDERS[part][phase]
        here = self.at[dim]
        right, left = lax.rem(here + 1, SIDE), lax.rem(here + SIDE - 1, SIDE)
        rows = self.shard.shape[0]
        for side, (peer, other) in enumerate(((right, left), (left, right))):
            if step == 0:
                piece = self.region(part, phase, here, pl.ds(0, rows))
            else:
                piece = self.region(part, phase, other, pl.ds(side * (rows // 2), rows // 2))
            yield pltpu.make_async_remote_copy(
                src_ref=piece,
                dst_ref=piece,
                send_sem=self.ring_send.at[part, phase, step, side],
                recv_sem=self.ring_recv.at[part, phase, step, side],
                device_id=self.device(dim, peer, self.core),
                device_id_type=MESH,
            )

    def pair(self, part, turn):
        dim = ORDERS[part][2]
        place = lax.rem(self.at[dim] + turn, SIDE)
        piece = self.region(part, 2, place, pl.ds(0, self.shard.shape[0]))
        return pltpu.make_async_remote_copy(
            src_ref=piece,
            dst_ref=piece,
            send_sem=self.pair_send.at[part, turn],
            recv_sem=self.pair_recv.at[part, turn],
            device_id=self.device(None, None, 1 - self.core),
            device_id_type=MESH,
        )

    def post(self, part, number):
        for copy in self.ring(part, number // 2, number % 2):
            copy.start()

    def begin(self):
        own = pltpu.make_async_copy(
            self.shard, self.whole.at[(*self.at, self.core)], self.own_sem.at[0]
        )
        own.start()
        own.wait()
        for part in range(3):
            self.post(part, 0)

    def advance(self, number):
        turns = {3: (0,), 4: (1, 3), 5: (2,)}.get(number, ())
        for part in range(3):
            for copy in self.ring(part, number // 2, number % 2):
                copy.wait()
            if number < 5:
                self.post(part, number + 1)
            for turn in turns:
                self.pair(part, turn).start()

    def end(self):
        for part in range(3):
            for turn in range(SIDE):
                self.pair(part, turn).wait()


def layer_kernel(
    n, scale, x, b, c, steps, cot, shard, out, grad_x, grad_b, grad_c,
    level, level_t, masked, masked_t, b_t, c_t, decays, y, send, recv, stage, before, mixed,
    whole, back, dshift, flow, inner_sum, b_sum, c_sum, send2, recv2, stage2, after,
    sems, own_sem, ring_send, ring_recv, pair_send, pair_recv,
):
    me = lax.axis_index("ctx")
    rows = x.shape[0]
    state = b.shape[1]
    barrier = greet_all(n)
    gather = Gather(shard, whole, own_sem, ring_send, ring_recv, pair_send, pair_recv)
    pl.semaphore_wait(barrier, n + 1)
    gather.begin()

    accumulate_decay(steps, level)
    level_t[...] = flip(level[...])
    row, column = grid_of(rows, rows)
    masked[...] = jnp.where(row >= column, scale * dot_nt(c[...], b[...]), 0.0)
    masked_t[...] = jnp.where(row <= column, scale * dot_nt(b[...], c[...]), 0.0)
    b_t[...] = flip(b[...]).astype(BF)
    c_t[...] = flip(c[...]).astype(BF)
    inner_sum[...] = jnp.zeros_like(inner_sum)
    b_sum[...] = jnp.zeros_like(b_sum)
    c_sum[...] = jnp.zeros_like(c_sum)

    def make_term(j, carry):
        both, last = paired(level, j)
        shifted = (x[:, span(j)].astype(F32) * jnp.exp2(both - last)).astype(BF)
        send[j, :state] = dot(b_t[...], shifted).astype(BF)
        d = jnp.exp2(-last)
        high = d.astype(BF).astype(F32)
        middle = (d - high).astype(BF).astype(F32)
        low = d - high - middle
        which, _ = grid_of(16, LANES)
        parts = jnp.where(which == 0, high, jnp.where(which == 1, middle, low))
        send[j, state:] = jnp.where(which < 3, parts, 0.0).astype(BF)
        return carry

    def inside(j, carry):
        one, two = columns_of(level, j)
        first = jnp.exp2(jnp.minimum(level_t[pl.ds(2 * j, 1), :] - one, 0.0))
        second = jnp.exp2(jnp.minimum(level_t[pl.ds(2 * j + 1, 1), :] - two, 0.0))
        mix = jnp.concatenate(
            [(masked[...] * first).astype(BF), (masked[...] * second).astype(BF)], axis=1
        )
        y[j] = dot(mix, split_heads(x[:, span(j)]))
        return carry

    gather.advance(0)
    lax.fori_loop(0, n // 4, make_term, 0)
    gather.advance(1)
    lax.fori_loop(n // 4, n, make_term, 0)
    gather.advance(2)
    lax.fori_loop(0, n // 4, inside, 0)
    gather.advance(3)

    def post_term(i, carry):
        j = lax.rem(me + i, n)
        copy_to(j, send.at[j], recv.at[me], sems, 0).start()
        return carry

    lax.fori_loop(1, n, post_term, 0)
    recv[me] = send[me]
    lax.fori_loop(n // 4, n, inside, 0)
    gather.advance(4)
    finish(n, send, recv, sems, 0)

    def step(k, carry):
        stage[k] = carry.astype(BF)
        parts = recv[k, state:].astype(F32)
        d = parts[0:1] + parts[1:2] + parts[2:3]
        decays[k] = jnp.broadcast_to(d, (8, LANES))

        @pl.when(k != me)
        def _():
            copy_to(k, stage.at[k], before.at[me], sems, 2).start()

        return d * carry + recv[k, :state].astype(F32)

    lax.fori_loop(0, n, step, jnp.zeros((state, LANES), F32))
    before[me] = stage[me]
    gather.advance(5)
    gather.end()

    depth = 2 * LANES

    def send_term(i, carry):
        q = lax.rem(me // 2 + 1 + i, n // 2)
        chunk = whole[q // SIDE, lax.rem(q, SIDE)].reshape(depth, cot.shape[1])
        part = dot_nt(cot[...], chunk).astype(BF)
        back[:, span(q, depth)] = part
        for u in range(2):
            j = q * 2 + u
            both, _ = paired(level, j)
            piece = part[:, u * LANES : (u + 1) * LANES].astype(F32)
            shift = (piece * jnp.exp2(-both)).astype(BF)
            dshift[:, span(j)] = shift
            send2[j] = dot(c_t[...], shift).astype(BF)

            @pl.when(j != me)
            def _():
                copy_to(j, send2.at[j], recv2.at[me], sems, 4).start()

        return carry

    lax.fori_loop(0, n // 2, send_term, 0)
    recv2[me] = send2[me]
    finish(n, stage, before, sems, 2)

    def inside_back(j, carry):
        one, two = columns_of(level, j)
        first = jnp.exp2(jnp.minimum(one - level_t[pl.ds(2 * j, 1), :], 0.0))
        second = jnp.exp2(jnp.minimum(two - level_t[pl.ds(2 * j + 1, 1), :], 0.0))
        mix = jnp.concatenate(
            [(masked_t[...] * first).astype(BF), (masked_t[...] * second).astype(BF)], axis=1
        )
        part = back[:, span(j)]
        flow[j] = dot(mix, split_heads(part))
        pair = dot_nt(split_heads(x[:, span(j)]), part)
        inner_sum[...] += first * pair[:rows] + second * pair[rows:]
        c_sum[...] += dot_nt(dshift[:, span(j)], before[j])
        return carry

    lax.fori_loop(0, n // 2, inside_back, 0)
    finish(n, send2, recv2, sems, 4)

    def step_back(i, carry):
        k = n - 1 - i
        stage2[k] = carry.astype(BF)

        @pl.when(k != me)
        def _():
            copy_to(k, stage2.at[k], after.at[me], sems, 6).start()

        return decays[k, 0:1] * carry + recv2[k].astype(F32)

    lax.fori_loop(0, n, step_back, jnp.zeros((state, LANES), F32))
    after[me] = stage2[me]
    lax.fori_loop(n // 2, n, inside_back, 0)

    def join(j, carry):
        both, _ = paired(level, j)
        carried = scale * jnp.exp2(-both) * dot(c[...], before[j])
        mixed[:, span(j)] = (y[j] + carried).astype(BF)
        return carry

    lax.fori_loop(0, n, join, 0)

    def project(i, carry):
        chunk = whole[:, :, :, :, :, span(i, 256)].reshape(x.shape[1], 256)
        out[:, span(i, 256)] = dot(mixed[...], chunk).astype(BF)
        return carry

    lax.fori_loop(0, out.shape[1] // 256, project, 0)
    kernel_t = jnp.where(row <= column, scale * inner_sum[...], 0.0)
    kernel = kernel_t.T.astype(BF)
    grad_c[...] = (dot(kernel, b[...]) + scale * c_sum[...]).astype(BF)
    finish(n, stage2, after, sems, 6)

    def join_back(j, carry):
        both, last = paired(level, j)
        tail = jnp.exp2(both - last)
        grad_x[:, span(j)] = (flow[j] + scale * tail * dot(b[...], after[j])).astype(BF)
        shifted = (x[:, span(j)].astype(F32) * tail).astype(BF)
        b_sum[...] += dot_nt(shifted, after[j])
        return carry

    lax.fori_loop(0, n, join_back, 0)
    grad_b[...] = (dot(kernel_t.astype(BF), c[...]) + scale * b_sum[...]).astype(BF)


def body(x_in, b_in, c_in, log_decay, w_out, cotangent):
    x, b, c, steps, cot = x_in[0], b_in[0], c_in[0], log_decay[0], cotangent[0]
    rows = x.shape[0]
    state = b.shape[1]
    n = lax.axis_size("ctx")
    scale = (state * rows * n) ** (-0.5)
    vmem = pl.BlockSpec(memory_space=pltpu.VMEM)
    shape = jax.ShapeDtypeStruct
    square = pltpu.VMEM((rows, rows), F32)
    turned = pltpu.VMEM((state, rows), BF)
    blocks = pltpu.VMEM((n, state, LANES), BF)
    marked = pltpu.VMEM((n, state + 16, LANES), BF)
    parts = pltpu.VMEM((n, rows, LANES), F32)
    wide = pltpu.VMEM(x.shape, BF)
    sums = pltpu.VMEM((rows, state), F32)
    ring = pltpu.SemaphoreType.DMA((3, 3, 2, 2))
    pair = pltpu.SemaphoreType.DMA((3, SIDE))
    results = pl.pallas_call(
        functools.partial(layer_kernel, n, scale),
        out_shape=(
            shape(cot.shape, BF), shape(x.shape, BF), shape(b.shape, BF), shape(c.shape, BF),
        ),
        in_specs=[vmem] * 6,
        out_specs=(vmem,) * 4,
        scratch_shapes=[
            square, square, square, square, turned, turned,
            pltpu.VMEM((n, 8, LANES), F32),
            parts, marked, marked, blocks, blocks, wide,
            pltpu.VMEM((SIDE, SIDE, SIDE, 2) + w_out.shape, BF),
            wide, wide, parts, square, sums, sums, blocks, blocks, blocks, blocks,
            pltpu.SemaphoreType.DMA((8,)),
            pltpu.SemaphoreType.DMA((1,)),
            ring, ring, pair, pair,
        ],
        compiler_params=pltpu.CompilerParams(
            collective_id=0, has_side_effects=True, vmem_limit_bytes=60 * 1024 * 1024
        ),
        name="layer",
    )(x, b, c, steps, cot, w_out)
    return tuple(r[None] for r in results)


def solution(mesh):
    tokens = P("dp", "ctx", None)
    return jax.shard_map(
        body,
        mesh=mesh,
        in_specs=(tokens, tokens, tokens, tokens, P(("dp", "ctx"), None), tokens),
        out_specs=(tokens, tokens, tokens, tokens),
        check_vma=False,
    )
```

time: 186 us -> 136 us (0.73)
  waiting for transfers between devices: 50.6 us -> 0 us
  Pallas kernels: 112 us -> 130 us
  between operations: 14 us -> 0.65 us
  local copies, waits for them, and re-layouts: 8.4 us -> 5.82 us
    all_gather x1 -> x0, waiting for transfers between devices: 49.9 us -> none  [body(): whole = lax.all_gather(w_out, ('dp', 'ctx'), axis=0, tiled=True)]
    pallas_call x2 -> x1, Pallas kernels: 112 us -> 130 us  [body(): pl.pallas_call(functools.partial(layer_kernel, n, scale), out_shape=(shap...]
    unnamed x5 -> x11, local copies, waits for them, and re-layouts: 8.4 us -> 5.82 us
  transfers between devices with their start and end apart: 1 -> 0, of which waited for: 1 -> 0; matrix products, arithmetic and copies ran while one was open for 1% -> 0% of each run, Pallas kernels for 27% -> 0%
where the time goes in v3:
time: 136 us
  Pallas kernels  130 us (96%)
  local copies, waits for them, and re-layouts  5.82 us (4%)
    pallas_call x1, Pallas kernels, body(): pl.pallas_call(functools.partial(layer_kernel, n, scale), out_shape=(shap...  130 us
    unnamed x11, local copies, waits for them, and re-layouts  5.82 us

profile of v3, /device:TPU:1, one launch (start us, length us, event | category | flops | bytes accessed | tf_op | source)
XLA Modules:
  0.0 136.1 jit_solution(1310550247461285994)
XLA Ops:
  0.6 1.5 %copy.10 = s32[1,128,64]{2,1,0:T(8,128)} copy(s32[1,128,64]{1,2,0:T(8,128)} %param.9) | data formatting | bytes 65536 | tf_op args[3]
  2.1 129.6 %layer.1 = (bf16[128,2048]{1,0:T(8,128)(2,1)}, bf16[128,4096]{1,0:T(8,128)(2,1)}, bf16[128,128]{1,0:T(8,128)(2,1)}, bf16[128,128]{1,0:T(8,128)(2,1)}) custom-call(bf16[128,4096]{1,0:T(8,128)(2,1)} %bitcast.9, bf16[128,128]{1,0:T(8,128)(2,1)} %bitcast.14, bf16[128,128]{1,0:T(8,128)(2,1)} %bitcast.15, s32[128,64]{1,0:T(8,128)} %bitcast.13, ...), custom_call_target="tpu_custom_call" | custom-call | tf_op jit(solution)/shard_map/layer/pallas_call | solution.py:383
  131.8 0.0 copy-start
  131.8 2.0 %copy.15 = bf16[1,128,2048]{2,1,0:T(8,128)(2,1)} copy(bf16[1,128,2048]{2,1,0:T(8,128)(2,1)} %bitcast.12) | data formatting | bytes 1048576
  133.7 0.0 copy-done
  133.8 0.0 copy-start.2
  133.8 1.0 copy.16
  134.7 0.0 copy-done.2
  134.7 0.0 copy-start.1
  134.7 0.6 copy.17
  135.3 0.2 copy-done.1
  135.5 0.6 copy.18
Async XLA Ops:
  131.8 2.0 %copy-start = (bf16[128,4096]{1,0:T(8,128)(2,1)S(1)}, bf16[128,4096]{1,0:T(8,128)(2,1)}, u32[]{:S(2)}) copy-start(bf16[128,4096]{1,0:T(8,128)(2,1)} %get-tuple-element.9) | copy-start | bytes 3145732
  133.8 1.0 copy-start.2
  134.7 0.8 copy-start.1

commit v4 on v3

--- a/solution.py
+++ b/solution.py
@@ -15,7 +15,9 @@
 LANES = 128
 SIDE = 4
 ORDERS = ((1, 0, 2), (0, 2, 1), (2, 1, 0))
-CUTS = (0, 640, 1280, 2048)
+CUTS = (0, 640, 1152, 2048)
+WIDE = 2 * LANES
+GROUP = 8
 
 
 def dot(a, b):
@@ -76,28 +78,34 @@
     copy_to(peer, source.at[some], target.at[some], sems, first).wait()
 
 
-def accumulate_decay(steps, level):
-    rows, heads = steps.shape
+def accumulate_decay(steps_t, level_t):
+    heads, rows = steps_t.shape
     row, column = grid_of(rows, rows)
-    ones = jnp.where(row >= column, 1.0, 0.0).astype(BF)
-    value = steps[...]
+    ones = jnp.where(row <= column, 1.0, 0.0).astype(BF)
+    value = steps_t[...]
     high = (value >> 7).astype(F32).astype(BF)
     low = (value & 127).astype(F32).astype(BF)
-    level[...] = jnp.zeros_like(level)
-    level[:, :heads] = (dot(ones, high) * 128.0 + dot(ones, low)) * rate
-
-
-def columns_of(level, j):
-    rolled = pltpu.roll(level[...], lax.rem(LANES - 2 * j, LANES), 1)
-    shape = rolled.shape
-    return jnp.broadcast_to(rolled[:, 0:1], shape), jnp.broadcast_to(rolled[:, 1:2], shape)
-
-
-def paired(level, j):
-    one, two = columns_of(level, j)
-    _, column = grid_of(*one.shape)
-    both = jnp.where(column < LANES // 2, one, two)
+    level_t[...] = jnp.zeros_like(level_t)
+    level_t[:heads, :] = (dot(high, ones) * 128.0 + dot(low, ones)) * rate
+
+
+def columns_of(level, q):
+    rolled = pltpu.roll(level[...], lax.rem(LANES - 4 * q, LANES), 1)
+    return [jnp.broadcast_to(rolled[:, i : i + 1], rolled.shape) for i in range(4)]
+
+
+def spread(level, q):
+    parts = columns_of(level, q)
+    _, column = grid_of(*parts[0].shape)
+    left = column < LANES // 2
+    both = jnp.concatenate(
+        [jnp.where(left, parts[0], parts[1]), jnp.where(left, parts[2], parts[3])], axis=1
+    )
     return both, both[both.shape[0] - 1 :]
+
+
+def beside(blocks, q):
+    return jnp.concatenate([blocks[2 * q], blocks[2 * q + 1]], axis=1)
 
 
 def split_heads(value):
@@ -193,9 +201,9 @@
 
 
 def layer_kernel(
-    n, scale, x, b, c, steps, cot, shard, out, grad_x, grad_b, grad_c,
+    n, scale, x, b, c, steps_t, cot, shard, out, grad_x, grad_b, grad_c,
     level, level_t, masked, masked_t, b_t, c_t, decays, y, send, recv, stage, before, mixed,
-    whole, back, dshift, flow, inner_sum, b_sum, c_sum, send2, recv2, stage2, after,
+    whole, back, dshift, flow, inner_sum, b_sum, c_sum, send2, recv2, stage2, after, falls, tails, shifts,
     sems, own_sem, ring_send, ring_recv, pair_send, pair_recv,
 ):
     me = lax.axis_index("ctx")
@@ -206,8 +214,8 @@
     pl.semaphore_wait(barrier, n + 1)
     gather.begin()
 
-    accumulate_decay(steps, level)
-    level_t[...] = flip(level[...])
+    accumulate_decay(steps_t, level_t)
+    level[...] = flip(level_t[...])
     row, column = grid_of(rows, rows)
     masked[...] = jnp.where(row >= column, scale * dot_nt(c[...], b[...]), 0.0)
     masked_t[...] = jnp.where(row <= column, scale * dot_nt(b[...], c[...]), 0.0)
@@ -217,35 +225,42 @@
     b_sum[...] = jnp.zeros_like(b_sum)
     c_sum[...] = jnp.zeros_like(c_sum)
 
-    def make_term(j, carry):
-        both, last = paired(level, j)
-        shifted = (x[:, span(j)].astype(F32) * jnp.exp2(both - last)).astype(BF)
-        send[j, :state] = dot(b_t[...], shifted).astype(BF)
+    def make_term(q, carry):
+        both, last = spread(level, q)
+        falls[q] = jnp.exp2(-both)
+        tail = jnp.exp2(both - last)
+        tails[q] = tail
+        shifted = (x[:, span(q, WIDE)].astype(F32) * tail).astype(BF)
+        shifts[:, span(q, WIDE)] = shifted
+        term = dot(b_t[...], shifted).astype(BF)
         d = jnp.exp2(-last)
         high = d.astype(BF).astype(F32)
         middle = (d - high).astype(BF).astype(F32)
         low = d - high - middle
-        which, _ = grid_of(16, LANES)
+        which, _ = grid_of(16, WIDE)
         parts = jnp.where(which == 0, high, jnp.where(which == 1, middle, low))
-        send[j, state:] = jnp.where(which < 3, parts, 0.0).astype(BF)
-        return carry
-
-    def inside(j, carry):
-        one, two = columns_of(level, j)
-        first = jnp.exp2(jnp.minimum(level_t[pl.ds(2 * j, 1), :] - one, 0.0))
-        second = jnp.exp2(jnp.minimum(level_t[pl.ds(2 * j + 1, 1), :] - two, 0.0))
-        mix = jnp.concatenate(
-            [(masked[...] * first).astype(BF), (masked[...] * second).astype(BF)], axis=1
-        )
-        y[j] = dot(mix, split_heads(x[:, span(j)]))
+        parts = jnp.where(which < 3, parts, 0.0).astype(BF)
+        for u in range(2):
+            send[2 * q + u, :state] = term[:, u * LANES : (u + 1) * LANES]
+            send[2 * q + u, state:] = parts[:, u * LANES : (u + 1) * LANES]
+        return carry
+
+    def inside(q, carry):
+        columns = columns_of(level, q)
+        for u in range(2):
+            mix = []
+            for v in (2 * u, 2 * u + 1):
+                gap = level_t[pl.ds(4 * q + v, 1), :] - columns[v]
+                mix.append((masked[...] * jnp.exp2(jnp.minimum(gap, 0.0))).astype(BF))
+            y[2 * q + u] = dot(jnp.concatenate(mix, axis=1), split_heads(x[:, span(2 * q + u)]))
         return carry
 
     gather.advance(0)
-    lax.fori_loop(0, n // 4, make_term, 0)
+    lax.fori_loop(0, n // 8, make_term, 0)
     gather.advance(1)
-    lax.fori_loop(n // 4, n, make_term, 0)
+    lax.fori_loop(n // 8, n // 2, make_term, 0)
     gather.advance(2)
-    lax.fori_loop(0, n // 4, inside, 0)
+    lax.fori_loop(0, n // 8, inside, 0)
     gather.advance(3)
 
     def post_term(i, carry):
@@ -255,90 +270,119 @@
 
     lax.fori_loop(1, n, post_term, 0)
     recv[me] = send[me]
-    lax.fori_loop(n // 4, n, inside, 0)
+    lax.fori_loop(n // 8, n // 2, inside, 0)
     gather.advance(4)
     finish(n, send, recv, sems, 0)
 
-    def step(k, carry):
-        stage[k] = carry.astype(BF)
-        parts = recv[k, state:].astype(F32)
-        d = parts[0:1] + parts[1:2] + parts[2:3]
-        decays[k] = jnp.broadcast_to(d, (8, LANES))
-
-        @pl.when(k != me)
-        def _():
-            copy_to(k, stage.at[k], before.at[me], sems, 2).start()
-
-        return d * carry + recv[k, :state].astype(F32)
-
-    lax.fori_loop(0, n, step, jnp.zeros((state, LANES), F32))
+    def step(g, carry):
+        for u in range(GROUP):
+            k = g * GROUP + u
+            stage[k] = carry.astype(BF)
+            parts = recv[k, state:].astype(F32)
+            d = parts[0:1] + parts[1:2] + parts[2:3]
+            decays[k] = jnp.broadcast_to(d, (8, LANES))
+            carry = d * carry + recv[k, :state].astype(F32)
+
+        def post(k, nothing):
+            @pl.when(k != me)
+            def _():
+                copy_to(k, stage.at[k], before.at[me], sems, 2).start()
+
+            return nothing
+
+        lax.fori_loop(g * GROUP, (g + 1) * GROUP, post, 0)
+        return carry
+
+    lax.fori_loop(0, n // GROUP, step, jnp.zeros((state, LANES), F32))
     before[me] = stage[me]
     gather.advance(5)
     gather.end()
 
-    depth = 2 * LANES
-
-    def send_term(i, carry):
-        q = lax.rem(me // 2 + 1 + i, n // 2)
-        chunk = whole[q // SIDE, lax.rem(q, SIDE)].reshape(depth, cot.shape[1])
-        part = dot_nt(cot[...], chunk).astype(BF)
-        back[:, span(q, depth)] = part
+    def place(i):
+        return lax.rem(me // 2 + 1 + i, n // 2)
+
+    def make_back(i):
+        q = place(i)
+        chunk = whole[q // SIDE, lax.rem(q, SIDE)].reshape(WIDE, cot.shape[1])
+        back[:, span(q, WIDE)] = dot_nt(cot[...], chunk).astype(BF)
+
+    def make_term_back(i):
+        q = place(i)
+        shift = (back[:, span(q, WIDE)].astype(F32) * falls[q]).astype(BF)
+        dshift[:, span(q, WIDE)] = shift
+        term = dot(c_t[...], shift).astype(BF)
         for u in range(2):
-            j = q * 2 + u
-            both, _ = paired(level, j)
-            piece = part[:, u * LANES : (u + 1) * LANES].astype(F32)
-            shift = (piece * jnp.exp2(-both)).astype(BF)
-            dshift[:, span(j)] = shift
-            send2[j] = dot(c_t[...], shift).astype(BF)
+            send2[2 * q + u] = term[:, u * LANES : (u + 1) * LANES]
+
+    def post_back(i):
+        for u in range(2):
+            j = place(i) * 2 + u
 
             @pl.when(j != me)
             def _():
                 copy_to(j, send2.at[j], recv2.at[me], sems, 4).start()
 
-        return carry
-
-    lax.fori_loop(0, n // 2, send_term, 0)
+    def send_term(i, carry):
+        make_term_back(i - 1)
+        make_back(i)
+        post_back(i - 1)
+        return carry
+
+    make_back(0)
+    lax.fori_loop(1, n // 2, send_term, 0)
+    make_term_back(n // 2 - 1)
+    post_back(n // 2 - 1)
     recv2[me] = send2[me]
     finish(n, stage, before, sems, 2)
 
-    def inside_back(j, carry):
-        one, two = columns_of(level, j)
-        first = jnp.exp2(jnp.minimum(one - level_t[pl.ds(2 * j, 1), :], 0.0))
-        second = jnp.exp2(jnp.minimum(two - level_t[pl.ds(2 * j + 1, 1), :], 0.0))
-        mix = jnp.concatenate(
-            [(masked_t[...] * first).astype(BF), (masked_t[...] * second).astype(BF)], axis=1
-        )
-        part = back[:, span(j)]
-        flow[j] = dot(mix, split_heads(part))
-        pair = dot_nt(split_heads(x[:, span(j)]), part)
-        inner_sum[...] += first * pair[:rows] + second * pair[rows:]
-        c_sum[...] += dot_nt(dshift[:, span(j)], before[j])
+    def inside_back(q, carry):
+        columns = columns_of(level, q)
+        total = inner_sum[...]
+        for u in range(2):
+            j = 2 * q + u
+            part = back[:, span(j)]
+            pair = dot_nt(split_heads(x[:, span(j)]), part)
+            mix = []
+            for v in range(2):
+                gap = columns[2 * u + v] - level_t[pl.ds(4 * q + 2 * u + v, 1), :]
+                fade = jnp.exp2(jnp.minimum(gap, 0.0))
+                mix.append((masked_t[...] * fade).astype(BF))
+                total = total + fade * pair[v * rows : (v + 1) * rows]
+            flow[j] = dot(jnp.concatenate(mix, axis=1), split_heads(part))
+        inner_sum[...] = total
+        c_sum[...] += dot_nt(dshift[:, span(q, WIDE)], beside(before, q))
         return carry
 
     lax.fori_loop(0, n // 2, inside_back, 0)
     finish(n, send2, recv2, sems, 4)
 
-    def step_back(i, carry):
-        k = n - 1 - i
-        stage2[k] = carry.astype(BF)
-
-        @pl.when(k != me)
-        def _():
-            copy_to(k, stage2.at[k], after.at[me], sems, 6).start()
-
-        return decays[k, 0:1] * carry + recv2[k].astype(F32)
-
-    lax.fori_loop(0, n, step_back, jnp.zeros((state, LANES), F32))
+    def step_back(g, carry):
+        for u in range(GROUP):
+            k = n - 1 - (g * GROUP + u)
+            stage2[k] = carry.astype(BF)
+            carry = decays[k, 0:1] * carry + recv2[k].astype(F32)
+
+        def post(i, nothing):
+            k = n - 1 - i
+
+            @pl.when(k != me)
+            def _():
+                copy_to(k, stage2.at[k], after.at[me], sems, 6).start()
+
+            return nothing
+
+        lax.fori_loop(g * GROUP, (g + 1) * GROUP, post, 0)
+        return carry
+
+    lax.fori_loop(0, n // GROUP, step_back, jnp.zeros((state, LANES), F32))
     after[me] = stage2[me]
-    lax.fori_loop(n // 2, n, inside_back, 0)
-
-    def join(j, carry):
-        both, _ = paired(level, j)
-        carried = scale * jnp.exp2(-both) * dot(c[...], before[j])
-        mixed[:, span(j)] = (y[j] + carried).astype(BF)
-        return carry
-
-    lax.fori_loop(0, n, join, 0)
+
+    def join(q, carry):
+        carried = scale * falls[q] * dot(c[...], beside(before, q))
+        mixed[:, span(q, WIDE)] = (beside(y, q) + carried).astype(BF)
+        return carry
+
+    lax.fori_loop(0, n // 2, join, 0)
 
     def project(i, carry):
         chunk = whole[:, :, :, :, :, span(i, 256)].reshape(x.shape[1], 256)
@@ -351,15 +395,14 @@
     grad_c[...] = (dot(kernel, b[...]) + scale * c_sum[...]).astype(BF)
     finish(n, stage2, after, sems, 6)
 
-    def join_back(j, carry):
-        both, last = paired(level, j)
-        tail = jnp.exp2(both - last)
-        grad_x[:, span(j)] = (flow[j] + scale * tail * dot(b[...], after[j])).astype(BF)
-        shifted = (x[:, span(j)].astype(F32) * tail).astype(BF)
-        b_sum[...] += dot_nt(shifted, after[j])
-        return carry
-
-    lax.fori_loop(0, n, join_back, 0)
+    def join_back(q, carry):
+        late = beside(after, q)
+        carried = scale * tails[q] * dot(b[...], late)
+        grad_x[:, span(q, WIDE)] = (beside(flow, q) + carried).astype(BF)
+        b_sum[...] += dot_nt(shifts[:, span(q, WIDE)], late)
+        return carry
+
+    lax.fori_loop(0, n // 2, join_back, 0)
     grad_b[...] = (dot(kernel_t.astype(BF), c[...]) + scale * b_sum[...]).astype(BF)
 
 
@@ -377,6 +420,7 @@
     marked = pltpu.VMEM((n, state + 16, LANES), BF)
     parts = pltpu.VMEM((n, rows, LANES), F32)
     wide = pltpu.VMEM(x.shape, BF)
+    spreads = pltpu.VMEM((n // 2, rows, WIDE), F32)
     sums = pltpu.VMEM((rows, state), F32)
     ring = pltpu.SemaphoreType.DMA((3, 3, 2, 2))
     pair = pltpu.SemaphoreType.DMA((3, SIDE))
@@ -393,6 +437,7 @@
             parts, marked, marked, blocks, blocks, wide,
             pltpu.VMEM((SIDE, SIDE, SIDE, 2) + w_out.shape, BF),
             wide, wide, parts, square, sums, sums, blocks, blocks, blocks, blocks,
+            spreads, spreads, wide,
             pltpu.SemaphoreType.DMA((8,)),
             pltpu.SemaphoreType.DMA((1,)),
             ring, ring, pair, pair,
@@ -401,7 +446,7 @@
             collective_id=0, has_side_effects=True, vmem_limit_bytes=60 * 1024 * 1024
         ),
         name="layer",
-    )(x, b, c, steps, cot, w_out)
+    )(x, b, c, steps.T, cot, w_out)
     return tuple(r[None] for r in results)
 
 

time: 136 us -> 126 us (0.926)
  Pallas kernels: 130 us -> 121 us
  local copies, waits for them, and re-layouts: 5.82 us -> 4.33 us
    pallas_call x1, Pallas kernels: 130 us -> 121 us  [body(): pl.pallas_call(functools.partial(layer_kernel, n, scale), out_shape=(shap...]
    unnamed x11 -> x10, local copies, waits for them, and re-layouts: 5.82 us -> 4.33 us
where the time goes in v4:
time: 126 us; the launch traced here: 125 us
  Pallas kernels  121 us (96%)
  local copies, waits for them, and re-layouts  4.33 us (3%)
    pallas_call x1, Pallas kernels, body(): pl.pallas_call(functools.partial(layer_kernel, n, scale), out_shape=(shap...  121 us
    unnamed x10, local copies, waits for them, and re-layouts  4.33 us

profile of v4, /device:TPU:1, one launch (start us, length us, event | category | flops | bytes accessed | tf_op | source)
XLA Modules:
  0.0 125.5 jit_solution(9965724335084254015)
XLA Ops:
  0.6 120.5 %layer.1 = (bf16[128,2048]{1,0:T(8,128)(2,1)}, bf16[128,4096]{1,0:T(8,128)(2,1)}, bf16[128,128]{1,0:T(8,128)(2,1)}, bf16[128,128]{1,0:T(8,128)(2,1)}) custom-call(bf16[128,4096]{1,0:T(8,128)(2,1)} %bitcast.11, bf16[128,128]{1,0:T(8,128)(2,1)} %bitcast.15, bf16[128,128]{1,0:T(8,128)(2,1)} %bitcast.16, s32[64,128]{1,0:T(8,128)} %bitcast.17, ...), custom_call_target="tpu_custom_call" | custom-call | tf_op jit(solution)/shard_map/layer/pallas_call | solution.py:427
  121.1 0.0 copy-start
  121.2 2.0 %copy.14 = bf16[1,128,2048]{2,1,0:T(8,128)(2,1)} copy(bf16[1,128,2048]{2,1,0:T(8,128)(2,1)} %bitcast.14) | data formatting | bytes 1048576
  123.1 0.0 copy-done
  123.1 0.0 copy-start.2
  123.1 1.0 copy.15
  124.1 0.0 copy-done.2
  124.1 0.0 copy-start.1
  124.1 0.6 copy.16
  124.7 0.2 copy-done.1
  124.9 0.6 copy.17
Async XLA Ops:
  121.1 2.0 %copy-start = (bf16[128,4096]{1,0:T(8,128)(2,1)S(1)}, bf16[128,4096]{1,0:T(8,128)(2,1)}, u32[]{:S(2)}) copy-start(bf16[128,4096]{1,0:T(8,128)(2,1)} %get-tuple-element.9) | copy-start | bytes 3145732
  123.1 1.0 copy-start.2
  124.1 0.8 copy-start.1

commit v5 on v4

--- a/solution.py
+++ b/solution.py
@@ -15,7 +15,7 @@
 LANES = 128
 SIDE = 4
 ORDERS = ((1, 0, 2), (0, 2, 1), (2, 1, 0))
-CUTS = (0, 640, 1152, 2048)
+CUTS = (0, 512, 1024, 2048)
 WIDE = 2 * LANES
 GROUP = 8
 
@@ -184,9 +184,9 @@
         for part in range(3):
             self.post(part, 0)
 
-    def advance(self, number):
+    def advance(self, number, parts=(0, 1, 2)):
         turns = {3: (0,), 4: (1, 3), 5: (2,)}.get(number, ())
-        for part in range(3):
+        for part in parts:
             for copy in self.ring(part, number // 2, number % 2):
                 copy.wait()
             if number < 5:
@@ -194,8 +194,8 @@
             for turn in turns:
                 self.pair(part, turn).start()
 
-    def end(self):
-        for part in range(3):
+    def end(self, parts):
+        for part in parts:
             for turn in range(SIDE):
                 self.pair(part, turn).wait()
 
@@ -295,16 +295,31 @@
 
     lax.fori_loop(0, n // GROUP, step, jnp.zeros((state, LANES), F32))
     before[me] = stage[me]
-    gather.advance(5)
-    gather.end()
+    gather.advance(5, (0, 1))
+    gather.end((0, 1))
 
     def place(i):
         return lax.rem(me // 2 + 1 + i, n // 2)
 
+    early, late = pl.ds(0, CUTS[2]), pl.ds(CUTS[2], CUTS[3] - CUTS[2])
+
+    def share(q, columns):
+        chunk = whole[q // SIDE, lax.rem(q, SIDE), :, :, :, columns]
+        return dot_nt(cot[:, columns], chunk.reshape(WIDE, chunk.shape[-1]))
+
+    def begin_back(q, carry):
+        part = share(q, early)
+        for u in range(2):
+            flow[2 * q + u] = part[:, u * LANES : (u + 1) * LANES]
+        return carry
+
+    lax.fori_loop(0, n // 2, begin_back, 0)
+    gather.advance(5, (2,))
+    gather.end((2,))
+
     def make_back(i):
         q = place(i)
-        chunk = whole[q // SIDE, lax.rem(q, SIDE)].reshape(WIDE, cot.shape[1])
-        back[:, span(q, WIDE)] = dot_nt(cot[...], chunk).astype(BF)
+        back[:, span(q, WIDE)] = (beside(flow, q) + share(q, late)).astype(BF)
 
     def make_term_back(i):
         q = place(i)

time: 126 us -> 122 us (0.968); the launches traced: 125 us -> 120 us
  Pallas kernels: 121 us -> 115 us
    pallas_call x1, Pallas kernels: 121 us -> 115 us  [body(): pl.pallas_call(functools.partial(layer_kernel, n, scale), out_shape=(shap...]
where the time goes in v5:
time: 122 us; the launch traced here: 120 us
  Pallas kernels  115 us (94%)
  local copies, waits for them, and re-layouts  4.33 us (4%)
    pallas_call x1, Pallas kernels, body(): pl.pallas_call(functools.partial(layer_kernel, n, scale), out_shape=(shap...  115 us
    unnamed x10, local copies, waits for them, and re-layouts  4.33 us

profile of v5, /device:TPU:1, one launch (start us, length us, event | category | flops | bytes accessed | tf_op | source)
XLA Modules:
  0.0 120.0 jit_solution(13002677016683078794)
XLA Ops:
  0.6 115.0 %layer.1 = (bf16[128,2048]{1,0:T(8,128)(2,1)}, bf16[128,4096]{1,0:T(8,128)(2,1)}, bf16[128,128]{1,0:T(8,128)(2,1)}, bf16[128,128]{1,0:T(8,128)(2,1)}) custom-call(bf16[128,4096]{1,0:T(8,128)(2,1)} %bitcast.11, bf16[128,128]{1,0:T(8,128)(2,1)} %bitcast.15, bf16[128,128]{1,0:T(8,128)(2,1)} %bitcast.16, s32[64,128]{1,0:T(8,128)} %bitcast.17, ...), custom_call_target="tpu_custom_call" | custom-call | tf_op jit(solution)/shard_map/layer/pallas_call | solution.py:442
  115.6 0.0 copy-start
  115.6 2.0 %copy.14 = bf16[1,128,2048]{2,1,0:T(8,128)(2,1)} copy(bf16[1,128,2048]{2,1,0:T(8,128)(2,1)} %bitcast.14) | data formatting | bytes 1048576
  117.6 0.0 copy-done
  117.6 0.0 copy-start.2
  117.6 1.0 copy.15
  118.6 0.0 copy-done.2
  118.6 0.0 copy-start.1
  118.6 0.6 copy.16
  119.2 0.2 copy-done.1
  119.4 0.6 copy.17
Async XLA Ops:
  115.6 2.0 %copy-start = (bf16[128,4096]{1,0:T(8,128)(2,1)S(1)}, bf16[128,4096]{1,0:T(8,128)(2,1)}, u32[]{:S(2)}) copy-start(bf16[128,4096]{1,0:T(8,128)(2,1)} %get-tuple-element.9) | copy-start | bytes 3145732
  117.6 1.0 copy-start.2
  118.6 0.8 copy-start.1

commit v6 on v5

--- a/solution.py
+++ b/solution.py
@@ -49,11 +49,14 @@
 
     def greet(i, carry):
         pl.semaphore_signal(
-            barrier, inc=1, device_id={"ctx": lax.rem(me + i, n)}, device_id_type=MESH
+            barrier, inc=1, device_id={"ctx": lax.rem(me + 2 * i, n)}, device_id_type=MESH
         )
         return carry
 
-    lax.fori_loop(1, n, greet, 0)
+    lax.fori_loop(1, n // 2, greet, 0)
+    pl.semaphore_signal(
+        barrier, inc=1, device_id={"ctx": me + 1 - 2 * lax.rem(me, 2)}, device_id_type=MESH
+    )
     for turn in (1, SIDE - 1):
         pl.semaphore_signal(
             barrier, inc=1, device_id={"dp": lax.rem(seq + turn, SIDE)}, device_id_type=MESH
@@ -73,9 +76,23 @@
 
 
 def finish(n, source, target, sems, first):
-    peer = lax.rem(lax.axis_index("ctx") + 1, n)
-    some = pl.ds(0, n - 1)
+    peer = lax.rem(lax.axis_index("ctx") + 2, n)
+    some = pl.ds(0, n // 2 - 1)
     copy_to(peer, source.at[some], target.at[some], sems, first).wait()
+
+
+def in_parts(d):
+    high = d.astype(BF).astype(F32)
+    middle = (d - high).astype(BF).astype(F32)
+    low = d - high - middle
+    which, _ = grid_of(16, d.shape[1])
+    parts = jnp.where(which == 0, high, jnp.where(which == 1, middle, low))
+    return jnp.where(which < 3, parts, 0.0).astype(BF)
+
+
+def from_parts(rows):
+    parts = rows.astype(F32)
+    return parts[0:1] + parts[1:2] + parts[2:3]
 
 
 def accumulate_decay(steps_t, level_t):
@@ -106,6 +123,10 @@
 
 def beside(blocks, q):
     return jnp.concatenate([blocks[2 * q], blocks[2 * q + 1]], axis=1)
+
+
+def both_of(slabs, q):
+    return jnp.concatenate([slabs[0, q], slabs[1, q]], axis=1)
 
 
 def split_heads(value):
@@ -202,16 +223,21 @@
 
 def layer_kernel(
     n, scale, x, b, c, steps_t, cot, shard, out, grad_x, grad_b, grad_c,
-    level, level_t, masked, masked_t, b_t, c_t, decays, y, send, recv, stage, before, mixed,
-    whole, back, dshift, flow, inner_sum, b_sum, c_sum, send2, recv2, stage2, after, falls, tails, shifts,
+    level, level_t, masked, masked_t, b_t, c_t, decays, y, send, near, joint, recv, stage, got, give, before, mixed,
+    whole, back, dshift, flow, inner_sum, b_sum, c_sum, send2, near2, joint2, recv2, stage2, got2, give2, after,
+    falls, tails, shifts,
     sems, own_sem, ring_send, ring_recv, pair_send, pair_recv,
 ):
     me = lax.axis_index("ctx")
     rows = x.shape[0]
     state = b.shape[1]
+    core, chip, chips = lax.rem(me, 2), me // 2, n // 2
+    partner = me + 1 - 2 * core
+    first = (1 - core).astype(F32)
+    second = 1.0 - first
     barrier = greet_all(n)
     gather = Gather(shard, whole, own_sem, ring_send, ring_recv, pair_send, pair_recv)
-    pl.semaphore_wait(barrier, n + 1)
+    pl.semaphore_wait(barrier, n // 2 + 2)
     gather.begin()
 
     accumulate_decay(steps_t, level_t)
@@ -233,16 +259,10 @@
         shifted = (x[:, span(q, WIDE)].astype(F32) * tail).astype(BF)
         shifts[:, span(q, WIDE)] = shifted
         term = dot(b_t[...], shifted).astype(BF)
-        d = jnp.exp2(-last)
-        high = d.astype(BF).astype(F32)
-        middle = (d - high).astype(BF).astype(F32)
-        low = d - high - middle
-        which, _ = grid_of(16, WIDE)
-        parts = jnp.where(which == 0, high, jnp.where(which == 1, middle, low))
-        parts = jnp.where(which < 3, parts, 0.0).astype(BF)
+        parts = in_parts(jnp.exp2(-last))
         for u in range(2):
-            send[2 * q + u, :state] = term[:, u * LANES : (u + 1) * LANES]
-            send[2 * q + u, state:] = parts[:, u * LANES : (u + 1) * LANES]
+            send[u, q, :state] = term[:, u * LANES : (u + 1) * LANES]
+            send[u, q, state:] = parts[:, u * LANES : (u + 1) * LANES]
         return carry
 
     def inside(q, carry):
@@ -259,42 +279,54 @@
     lax.fori_loop(0, n // 8, make_term, 0)
     gather.advance(1)
     lax.fori_loop(n // 8, n // 2, make_term, 0)
+    near_terms = copy_to(partner, send.at[1 - core], near, sems, 0)
+    near_terms.start()
     gather.advance(2)
     lax.fori_loop(0, n // 8, inside, 0)
+    near_terms.wait()
+
+    def combine(q, carry):
+        mine, theirs = from_parts(send[core, q, state:]), from_parts(near[q, state:])
+        here = (first * theirs + second) * send[core, q, :state].astype(F32)
+        there = (second * mine + first) * near[q, :state].astype(F32)
+        joint[q, :state] = (here + there).astype(BF)
+        joint[q, state:] = in_parts(mine * theirs)
+        return carry
+
+    lax.fori_loop(0, chips, combine, 0)
     gather.advance(3)
 
     def post_term(i, carry):
-        j = lax.rem(me + i, n)
-        copy_to(j, send.at[j], recv.at[me], sems, 0).start()
-        return carry
-
-    lax.fori_loop(1, n, post_term, 0)
-    recv[me] = send[me]
+        q = lax.rem(chip + i, chips)
+        copy_to(2 * q + core, joint.at[q], recv.at[chip], sems, 2).start()
+        return carry
+
+    lax.fori_loop(1, chips, post_term, 0)
+    recv[chip] = joint[chip]
     lax.fori_loop(n // 8, n // 2, inside, 0)
     gather.advance(4)
-    finish(n, send, recv, sems, 0)
+    finish(n, joint, recv, sems, 2)
 
     def step(g, carry):
         for u in range(GROUP):
             k = g * GROUP + u
             stage[k] = carry.astype(BF)
-            parts = recv[k, state:].astype(F32)
-            d = parts[0:1] + parts[1:2] + parts[2:3]
+            d = from_parts(recv[k, state:])
             decays[k] = jnp.broadcast_to(d, (8, LANES))
             carry = d * carry + recv[k, :state].astype(F32)
 
         def post(k, nothing):
-            @pl.when(k != me)
+            @pl.when(k != chip)
             def _():
-                copy_to(k, stage.at[k], before.at[me], sems, 2).start()
+                copy_to(2 * k + core, stage.at[k], got.at[chip], sems, 4).start()
 
             return nothing
 
         lax.fori_loop(g * GROUP, (g + 1) * GROUP, post, 0)
         return carry
 
-    lax.fori_loop(0, n // GROUP, step, jnp.zeros((state, LANES), F32))
-    before[me] = stage[me]
+    lax.fori_loop(0, chips // GROUP, step, jnp.zeros((state, LANES), F32))
+    got[chip] = stage[chip]
     gather.advance(5, (0, 1))
     gather.end((0, 1))
 
@@ -314,6 +346,20 @@
         return carry
 
     lax.fori_loop(0, n // 2, begin_back, 0)
+    finish(n, stage, got, sems, 4)
+
+    def pass_on(q, carry):
+        early_state = got[q].astype(F32)
+        d = first * from_parts(send[core, q, state:]) + second * from_parts(near[q, state:])
+        term = first * send[core, q, :state].astype(F32) + second * near[q, :state].astype(F32)
+        late_state = d * early_state + term
+        before[core, q] = (first * early_state + second * late_state).astype(BF)
+        give[q] = (first * late_state + second * early_state).astype(BF)
+        return carry
+
+    lax.fori_loop(0, chips, pass_on, 0)
+    near_states = copy_to(partner, give, before.at[core], sems, 6)
+    near_states.start()
     gather.advance(5, (2,))
     gather.end((2,))
 
@@ -327,15 +373,11 @@
         dshift[:, span(q, WIDE)] = shift
         term = dot(c_t[...], shift).astype(BF)
         for u in range(2):
-            send2[2 * q + u] = term[:, u * LANES : (u + 1) * LANES]
+            send2[u, q] = term[:, u * LANES : (u + 1) * LANES]
 
     def post_back(i):
-        for u in range(2):
-            j = place(i) * 2 + u
-
-            @pl.when(j != me)
-            def _():
-                copy_to(j, send2.at[j], recv2.at[me], sems, 4).start()
+        q = place(i)
+        copy_to(partner, send2.at[1 - core, q], near2.at[q], sems, 8).start()
 
     def send_term(i, carry):
         make_term_back(i - 1)
@@ -347,8 +389,24 @@
     lax.fori_loop(1, n // 2, send_term, 0)
     make_term_back(n // 2 - 1)
     post_back(n // 2 - 1)
-    recv2[me] = send2[me]
-    finish(n, stage, before, sems, 2)
+    copy_to(partner, send2.at[1 - core], near2, sems, 8).wait()
+
+    def combine_back(i, carry):
+        q = lax.rem(chip + 1 + i, chips)
+        mine, theirs = from_parts(send[core, q, state:]), from_parts(near[q, state:])
+        here = (first + second * theirs) * send2[core, q].astype(F32)
+        there = (first * mine + second) * near2[q].astype(F32)
+        joint2[q] = (here + there).astype(BF)
+
+        @pl.when(q != chip)
+        def _():
+            copy_to(2 * q + core, joint2.at[q], recv2.at[chip], sems, 10).start()
+
+        return carry
+
+    lax.fori_loop(0, chips, combine_back, 0)
+    recv2[chip] = joint2[chip]
+    near_states.wait()
 
     def inside_back(q, carry):
         columns = columns_of(level, q)
@@ -365,39 +423,54 @@
                 total = total + fade * pair[v * rows : (v + 1) * rows]
             flow[j] = dot(jnp.concatenate(mix, axis=1), split_heads(part))
         inner_sum[...] = total
-        c_sum[...] += dot_nt(dshift[:, span(q, WIDE)], beside(before, q))
+        c_sum[...] += dot_nt(dshift[:, span(q, WIDE)], both_of(before, q))
         return carry
 
     lax.fori_loop(0, n // 2, inside_back, 0)
-    finish(n, send2, recv2, sems, 4)
+    finish(n, joint2, recv2, sems, 10)
 
     def step_back(g, carry):
         for u in range(GROUP):
-            k = n - 1 - (g * GROUP + u)
+            k = chips - 1 - (g * GROUP + u)
             stage2[k] = carry.astype(BF)
             carry = decays[k, 0:1] * carry + recv2[k].astype(F32)
 
         def post(i, nothing):
-            k = n - 1 - i
-
-            @pl.when(k != me)
+            k = chips - 1 - i
+
+            @pl.when(k != chip)
             def _():
-                copy_to(k, stage2.at[k], after.at[me], sems, 6).start()
+                copy_to(2 * k + core, stage2.at[k], got2.at[chip], sems, 12).start()
 
             return nothing
 
         lax.fori_loop(g * GROUP, (g + 1) * GROUP, post, 0)
         return carry
 
-    lax.fori_loop(0, n // GROUP, step_back, jnp.zeros((state, LANES), F32))
-    after[me] = stage2[me]
+    lax.fori_loop(0, chips // GROUP, step_back, jnp.zeros((state, LANES), F32))
+    got2[chip] = stage2[chip]
 
     def join(q, carry):
-        carried = scale * falls[q] * dot(c[...], beside(before, q))
+        carried = scale * falls[q] * dot(c[...], both_of(before, q))
         mixed[:, span(q, WIDE)] = (beside(y, q) + carried).astype(BF)
         return carry
 
     lax.fori_loop(0, n // 2, join, 0)
+
+    finish(n, stage2, got2, sems, 12)
+
+    def pass_back(q, carry):
+        late_state = got2[q].astype(F32)
+        d = first * from_parts(near[q, state:]) + second * from_parts(send[core, q, state:])
+        term = first * near2[q].astype(F32) + second * send2[core, q].astype(F32)
+        early_state = d * late_state + term
+        after[core, q] = (first * early_state + second * late_state).astype(BF)
+        give2[q] = (first * late_state + second * early_state).astype(BF)
+        return carry
+
+    lax.fori_loop(0, chips, pass_back, 0)
+    near_after = copy_to(partner, give2, after.at[core], sems, 14)
+    near_after.start()
 
     def project(i, carry):
         chunk = whole[:, :, :, :, :, span(i, 256)].reshape(x.shape[1], 256)
@@ -408,10 +481,10 @@
     kernel_t = jnp.where(row <= column, scale * inner_sum[...], 0.0)
     kernel = kernel_t.T.astype(BF)
     grad_c[...] = (dot(kernel, b[...]) + scale * c_sum[...]).astype(BF)
-    finish(n, stage2, after, sems, 6)
+    near_after.wait()
 
     def join_back(q, carry):
-        late = beside(after, q)
+        late = both_of(after, q)
         carried = scale * tails[q] * dot(b[...], late)
         grad_x[:, span(q, WIDE)] = (beside(flow, q) + carried).astype(BF)
         b_sum[...] += dot_nt(shifts[:, span(q, WIDE)], late)
@@ -431,8 +504,10 @@
     shape = jax.ShapeDtypeStruct
     square = pltpu.VMEM((rows, rows), F32)
     turned = pltpu.VMEM((state, rows), BF)
-    blocks = pltpu.VMEM((n, state, LANES), BF)
-    marked = pltpu.VMEM((n, state + 16, LANES), BF)
+    blocks = pltpu.VMEM((n // 2, state, LANES), BF)
+    marked = pltpu.VMEM((n // 2, state + 16, LANES), BF)
+    slabs = pltpu.VMEM((2, n // 2, state, LANES), BF)
+    marked_slabs = pltpu.VMEM((2, n // 2, state + 16, LANES), BF)
     parts = pltpu.VMEM((n, rows, LANES), F32)
     wide = pltpu.VMEM(x.shape, BF)
     spreads = pltpu.VMEM((n // 2, rows, WIDE), F32)
@@ -448,12 +523,13 @@
         out_specs=(vmem,) * 4,
         scratch_shapes=[
             square, square, square, square, turned, turned,
-            pltpu.VMEM((n, 8, LANES), F32),
-            parts, marked, marked, blocks, blocks, wide,
+            pltpu.VMEM((n // 2, 8, LANES), F32),
+            parts, marked_slabs, marked, marked, marked, blocks, blocks, blocks, slabs, wide,
             pltpu.VMEM((SIDE, SIDE, SIDE, 2) + w_out.shape, BF),
-            wide, wide, parts, square, sums, sums, blocks, blocks, blocks, blocks,
+            wide, wide, parts, square, sums, sums,
+            slabs, blocks, blocks, blocks, blocks, blocks, blocks, slabs,
             spreads, spreads, wide,
-            pltpu.SemaphoreType.DMA((8,)),
+            pltpu.SemaphoreType.DMA((16,)),
             pltpu.SemaphoreType.DMA((1,)),
             ring, ring, pair, pair,
         ],

time: 122 us -> 108 us (0.89)
  Pallas kernels: 115 us -> 102 us
    pallas_call x1, Pallas kernels: 115 us -> 102 us  [body(): pl.pallas_call(functools.partial(layer_kernel, n, scale), out_shape=(shap...]
where the time goes in v6:
time: 108 us; the launch traced here: 107 us
  Pallas kernels  102 us (94%)
  local copies, waits for them, and re-layouts  4.33 us (4%)
    pallas_call x1, Pallas kernels, body(): pl.pallas_call(functools.partial(layer_kernel, n, scale), out_shape=(shap...  102 us
    unnamed x10, local copies, waits for them, and re-layouts  4.33 us

profile of v6, /device:TPU:1, one launch (start us, length us, event | category | flops | bytes accessed | tf_op | source)
XLA Modules:
  0.0 107.1 jit_solution(15859579387331560354)
XLA Ops:
  0.6 102.1 %layer.1 = (bf16[128,2048]{1,0:T(8,128)(2,1)}, bf16[128,4096]{1,0:T(8,128)(2,1)}, bf16[128,128]{1,0:T(8,128)(2,1)}, bf16[128,128]{1,0:T(8,128)(2,1)}) custom-call(bf16[128,4096]{1,0:T(8,128)(2,1)} %bitcast.11, bf16[128,128]{1,0:T(8,128)(2,1)} %bitcast.15, bf16[128,128]{1,0:T(8,128)(2,1)} %bitcast.16, s32[64,128]{1,0:T(8,128)} %bitcast.17, ...), custom_call_target="tpu_custom_call" | custom-call | tf_op jit(solution)/shard_map/layer/pallas_call | solution.py:517
  102.8 0.0 copy-start
  102.8 2.0 %copy.14 = bf16[1,128,2048]{2,1,0:T(8,128)(2,1)} copy(bf16[1,128,2048]{2,1,0:T(8,128)(2,1)} %bitcast.14) | data formatting | bytes 1048576
  104.7 0.0 copy-done
  104.7 0.0 copy-start.2
  104.8 1.0 copy.15
  105.7 0.0 copy-done.2
  105.7 0.0 copy-start.1
  105.7 0.6 copy.16
  106.3 0.2 copy-done.1
  106.5 0.6 copy.17
Async XLA Ops:
  102.8 2.0 %copy-start = (bf16[128,4096]{1,0:T(8,128)(2,1)S(1)}, bf16[128,4096]{1,0:T(8,128)(2,1)}, u32[]{:S(2)}) copy-start(bf16[128,4096]{1,0:T(8,128)(2,1)} %get-tuple-element.9) | copy-start | bytes 3145732
  104.7 1.0 copy-start.2
  105.7 0.8 copy-start.1

commit v7 on v6

--- a/solution.py
+++ b/solution.py
@@ -215,9 +215,9 @@
             for turn in turns:
                 self.pair(part, turn).start()
 
-    def end(self, parts):
+    def end(self, parts, turns=range(SIDE)):
         for part in parts:
-            for turn in range(SIDE):
+            for turn in turns:
                 self.pair(part, turn).wait()
 
 
@@ -283,6 +283,7 @@
     near_terms.start()
     gather.advance(2)
     lax.fori_loop(0, n // 8, inside, 0)
+    gather.advance(3)
     near_terms.wait()
 
     def combine(q, carry):
@@ -294,7 +295,6 @@
         return carry
 
     lax.fori_loop(0, chips, combine, 0)
-    gather.advance(3)
 
     def post_term(i, carry):
         q = lax.rem(chip + i, chips)
@@ -331,7 +331,9 @@
     gather.end((0, 1))
 
     def place(i):
-        return lax.rem(me // 2 + 1 + i, n // 2)
+        row = i // SIDE
+        turn = row + (row // 2) * (5 - 2 * row)
+        return lax.rem(lax.axis_index("dp") + turn, SIDE) * SIDE + lax.rem(i, SIDE)
 
     early, late = pl.ds(0, CUTS[2]), pl.ds(CUTS[2], CUTS[3] - CUTS[2])
 
@@ -360,8 +362,7 @@
     lax.fori_loop(0, chips, pass_on, 0)
     near_states = copy_to(partner, give, before.at[core], sems, 6)
     near_states.start()
-    gather.advance(5, (2,))
-    gather.end((2,))
+    gather.end((2,), (0, 1, 3))
 
     def make_back(i):
         q = place(i)
@@ -386,7 +387,11 @@
         return carry
 
     make_back(0)
-    lax.fori_loop(1, n // 2, send_term, 0)
+    lax.fori_loop(1, 2 * SIDE, send_term, 0)
+    gather.advance(5, (2,))
+    lax.fori_loop(2 * SIDE, 3 * SIDE, send_term, 0)
+    gather.end((2,), (2,))
+    lax.fori_loop(3 * SIDE, n // 2, send_term, 0)
     make_term_back(n // 2 - 1)
     post_back(n // 2 - 1)
     copy_to(partner, send2.at[1 - core], near2, sems, 8).wait()

time: 108 us -> 106 us (0.981)
  Pallas kernels: 102 us -> 100 us
    pallas_call x1, Pallas kernels: 102 us -> 100 us  [body(): pl.pallas_call(functools.partial(layer_kernel, n, scale), out_shape=(shap...]
where the time goes in v7:
time: 106 us; the launch traced here: 105 us
  Pallas kernels  100 us (94%)
  local copies, waits for them, and re-layouts  4.33 us (4%)
    pallas_call x1, Pallas kernels, body(): pl.pallas_call(functools.partial(layer_kernel, n, scale), out_shape=(shap...  100 us
    unnamed x10, local copies, waits for them, and re-layouts  4.33 us

profile of v7, /device:TPU:1, one launch (start us, length us, event | category | flops | bytes accessed | tf_op | source)
XLA Modules:
  0.0 105.1 jit_solution(231858749872316422)
XLA Ops:
  0.6 100.1 %layer.1 = (bf16[128,2048]{1,0:T(8,128)(2,1)}, bf16[128,4096]{1,0:T(8,128)(2,1)}, bf16[128,128]{1,0:T(8,128)(2,1)}, bf16[128,128]{1,0:T(8,128)(2,1)}) custom-call(bf16[128,4096]{1,0:T(8,128)(2,1)} %bitcast.11, bf16[128,128]{1,0:T(8,128)(2,1)} %bitcast.15, bf16[128,128]{1,0:T(8,128)(2,1)} %bitcast.16, s32[64,128]{1,0:T(8,128)} %bitcast.17, ...), custom_call_target="tpu_custom_call" | custom-call | tf_op jit(solution)/shard_map/layer/pallas_call | solution.py:522
  100.8 0.0 copy-start
  100.8 2.0 %copy.14 = bf16[1,128,2048]{2,1,0:T(8,128)(2,1)} copy(bf16[1,128,2048]{2,1,0:T(8,128)(2,1)} %bitcast.14) | data formatting | bytes 1048576
  102.7 0.0 copy-done
  102.7 0.0 copy-start.2
  102.7 1.0 copy.15
  103.7 0.0 copy-done.2
  103.7 0.0 copy-start.1
  103.7 0.6 copy.16
  104.3 0.2 copy-done.1
  104.5 0.6 copy.17
Async XLA Ops:
  100.8 2.0 %copy-start = (bf16[128,4096]{1,0:T(8,128)(2,1)S(1)}, bf16[128,4096]{1,0:T(8,128)(2,1)}, u32[]{:S(2)}) copy-start(bf16[128,4096]{1,0:T(8,128)(2,1)} %get-tuple-element.9) | copy-start | bytes 3145732
  102.7 1.0 copy-start.2
  103.7 0.8 copy-start.1

commit v8 on v7

--- a/solution.py
+++ b/solution.py
@@ -431,7 +431,8 @@
         c_sum[...] += dot_nt(dshift[:, span(q, WIDE)], both_of(before, q))
         return carry
 
-    lax.fori_loop(0, n // 2, inside_back, 0)
+    held = n // 2 - 5
+    lax.fori_loop(0, held, inside_back, 0)
     finish(n, joint2, recv2, sems, 10)
 
     def step_back(g, carry):
@@ -454,6 +455,7 @@
 
     lax.fori_loop(0, chips // GROUP, step_back, jnp.zeros((state, LANES), F32))
     got2[chip] = stage2[chip]
+    lax.fori_loop(held, n // 2, inside_back, 0)
 
     def join(q, carry):
         carried = scale * falls[q] * dot(c[...], both_of(before, q))
@@ -462,6 +464,13 @@
 
     lax.fori_loop(0, n // 2, join, 0)
 
+    def project(i, carry):
+        chunk = whole[:, :, :, :, :, span(i, WIDE)].reshape(x.shape[1], WIDE)
+        out[:, span(i, WIDE)] = dot(mixed[...], chunk).astype(BF)
+        return carry
+
+    tiles = out.shape[1] // WIDE
+    lax.fori_loop(0, 2, project, 0)
     finish(n, stage2, got2, sems, 12)
 
     def pass_back(q, carry):
@@ -477,12 +486,7 @@
     near_after = copy_to(partner, give2, after.at[core], sems, 14)
     near_after.start()
 
-    def project(i, carry):
-        chunk = whole[:, :, :, :, :, span(i, 256)].reshape(x.shape[1], 256)
-        out[:, span(i, 256)] = dot(mixed[...], chunk).astype(BF)
-        return carry
-
-    lax.fori_loop(0, out.shape[1] // 256, project, 0)
+    lax.fori_loop(2, tiles, project, 0)
     kernel_t = jnp.where(row <= column, scale * inner_sum[...], 0.0)
     kernel = kernel_t.T.astype(BF)
     grad_c[...] = (dot(kernel, b[...]) + scale * c_sum[...]).astype(BF)

time: 106 us -> 105 us (level)
  no operation moved by 1% of the time
where the time goes in v8:
time: 105 us; the launch traced here: 104 us
  Pallas kernels  99.2 us (94%)
  local copies, waits for them, and re-layouts  4.33 us (4%)
    pallas_call x1, Pallas kernels, body(): pl.pallas_call(functools.partial(layer_kernel, n, scale), out_shape=(shap...  99.2 us
    unnamed x10, local copies, waits for them, and re-layouts  4.33 us

profile of v8, /device:TPU:1, one launch (start us, length us, event | category | flops | bytes accessed | tf_op | source)
XLA Modules:
  0.0 104.1 jit_solution(3180183006814204653)
XLA Ops:
  0.6 99.2 %layer.1 = (bf16[128,2048]{1,0:T(8,128)(2,1)}, bf16[128,4096]{1,0:T(8,128)(2,1)}, bf16[128,128]{1,0:T(8,128)(2,1)}, bf16[128,128]{1,0:T(8,128)(2,1)}) custom-call(bf16[128,4096]{1,0:T(8,128)(2,1)} %bitcast.11, bf16[128,128]{1,0:T(8,128)(2,1)} %bitcast.15, bf16[128,128]{1,0:T(8,128)(2,1)} %bitcast.16, s32[64,128]{1,0:T(8,128)} %bitcast.17, ...), custom_call_target="tpu_custom_call" | custom-call | tf_op jit(solution)/shard_map/layer/pallas_call | solution.py:526
  99.8 0.0 copy-start
  99.8 2.0 %copy.14 = bf16[1,128,2048]{2,1,0:T(8,128)(2,1)} copy(bf16[1,128,2048]{2,1,0:T(8,128)(2,1)} %bitcast.14) | data formatting | bytes 1048576
  101.8 0.0 copy-done
  101.8 0.0 copy-start.2
  101.8 1.0 copy.15
  102.7 0.0 copy-done.2
  102.8 0.0 copy-start.1
  102.8 0.6 copy.16
  103.4 0.2 copy-done.1
  103.5 0.6 copy.17
Async XLA Ops:
  99.8 2.0 %copy-start = (bf16[128,4096]{1,0:T(8,128)(2,1)S(1)}, bf16[128,4096]{1,0:T(8,128)(2,1)}, u32[]{:S(2)}) copy-start(bf16[128,4096]{1,0:T(8,128)(2,1)} %get-tuple-element.9) | copy-start | bytes 3145732
  101.8 1.0 copy-start.2
  102.8 0.8 copy-start.1

commit v9 on v8

--- a/solution.py
+++ b/solution.py
@@ -304,7 +304,7 @@
     lax.fori_loop(1, chips, post_term, 0)
     recv[chip] = joint[chip]
     lax.fori_loop(n // 8, n // 2, inside, 0)
-    gather.advance(4)
+    gather.advance(4, (0, 1))
     finish(n, joint, recv, sems, 2)
 
     def step(g, carry):
@@ -328,6 +328,7 @@
     lax.fori_loop(0, chips // GROUP, step, jnp.zeros((state, LANES), F32))
     got[chip] = stage[chip]
     gather.advance(5, (0, 1))
+    gather.advance(4, (2,))
     gather.end((0, 1))
 
     def place(i):

time: 105 us -> 102 us (0.971)
  Pallas kernels: 99.2 us -> 96.5 us
    pallas_call x1, Pallas kernels: 99.2 us -> 96.5 us  [body(): pl.pallas_call(functools.partial(layer_kernel, n, scale), out_shape=(shap...]
where the time goes in v9:
time: 102 us; the launch traced here: 101 us
  Pallas kernels  96.5 us (95%)
  local copies, waits for them, and re-layouts  4.33 us (4%)
    pallas_call x1, Pallas kernels, body(): pl.pallas_call(functools.partial(layer_kernel, n, scale), out_shape=(shap...  96.5 us
    unnamed x10, local copies, waits for them, and re-layouts  4.33 us

profile of v9, /device:TPU:1, one launch (start us, length us, event | category | flops | bytes accessed | tf_op | source)
XLA Modules:
  0.0 101.5 jit_solution(10403210820982825437)
XLA Ops:
  0.6 96.5 %layer.1 = (bf16[128,2048]{1,0:T(8,128)(2,1)}, bf16[128,4096]{1,0:T(8,128)(2,1)}, bf16[128,128]{1,0:T(8,128)(2,1)}, bf16[128,128]{1,0:T(8,128)(2,1)}) custom-call(bf16[128,4096]{1,0:T(8,128)(2,1)} %bitcast.11, bf16[128,128]{1,0:T(8,128)(2,1)} %bitcast.15, bf16[128,128]{1,0:T(8,128)(2,1)} %bitcast.16, s32[64,128]{1,0:T(8,128)} %bitcast.17, ...), custom_call_target="tpu_custom_call" | custom-call | tf_op jit(solution)/shard_map/layer/pallas_call | solution.py:527
  97.1 0.0 copy-start
  97.2 2.0 %copy.14 = bf16[1,128,2048]{2,1,0:T(8,128)(2,1)} copy(bf16[1,128,2048]{2,1,0:T(8,128)(2,1)} %bitcast.14) | data formatting | bytes 1048576
  99.1 0.0 copy-done
  99.1 0.0 copy-start.2
  99.1 1.0 copy.15
  100.1 0.0 copy-done.2
  100.1 0.0 copy-start.1
  100.1 0.6 copy.16
  100.7 0.2 copy-done.1
  100.9 0.6 copy.17
Async XLA Ops:
  97.1 2.0 %copy-start = (bf16[128,4096]{1,0:T(8,128)(2,1)S(1)}, bf16[128,4096]{1,0:T(8,128)(2,1)}, u32[]{:S(2)}) copy-start(bf16[128,4096]{1,0:T(8,128)(2,1)} %get-tuple-element.9) | copy-start | bytes 3145732
  99.1 1.0 copy-start.2
  100.1 0.8 copy-start.1
